TPU v7x, 128 devices: a whole 4x4x4 slice. The times are simulated.
128 devices in a mesh: sfc: 16 (over y, x), grp: 8 (over z, core).
Axes of the slice: x: 4, y: 4, z: 4, core: 2. Of those that a mesh axis runs over, the one named last changes fastest.
Arguments:
- bin_points: float32 [131072, 5, 256], P(('sfc', 'grp')), may hold values from -1 to 1, as said below
- bin_plan: int32 [131072, 1], P(('sfc', 'grp')), may hold values from 0 to 15; in each aligned block of 1024 rows (0 to 1023, 1024 to 2047, ...) at most 128 rows name the same one
- bin_leaf: int32 [131072], P(('sfc', 'grp')), may hold values from 0 to 255
- leaf_slots: int32 [16, 8, 256], P('sfc', None, 'grp'), may hold values from 0 to 255, each once within a row
- box_slots: int32 [16, 8, 32], P('sfc'), may hold values from 0 to 31, each once within a row
- parent_cone: int32 [16, 256], P('sfc'), may hold values from 0 to 15
- box_cone: int32 [16, 32], P('sfc'), may hold values from 0 to 15
- cone_angles: float32 [16, 2], replicated, may hold values from -3.140625 to 3.140625
Outputs:
- leaf_expansions: float32 [32768, 2, 512], P(('sfc', 'grp'))
- level_one: float32 [4096, 2, 512], P(('sfc', 'grp'))
- level_two: float32 [512, 2, 512], P(('sfc', 'grp'))
Inputs may be any that keep to these rules, and one draw needn't show every extreme that they name: `bin_plan`: among the rows of one device no value is named by more than 128 rows, a bound that some block reaches. Each row leaf_slots[s, o, :] names every level-one box of segment s once, so every level-one box has exactly one child of each octant. Each row box_slots[s, o, :] names every level-two box of segment s once. `bin_points`: coordinates lie within -1 to 1 and densities within -0.4 to 0.4.
All inputs are finite; a program needn't handle non-finite values.
Results may differ from a plain program's by a relative error of at most 0.0039.
Values sent between devices are 32-bit elements; how exact they have to be, the bound alone decides.
No kernel may reach another device: no remote copies, remote signals or barrier semaphores. Data moves between devices by JAX's collectives and lax.ppermute only.
A program may use at most 320 MiB of HBM per device.

v0:
```python
import functools

import jax
import jax.numpy as jnp
import numpy as np
from jax import lax
from jax.experimental import pallas as pl
from jax.experimental.pallas import tpu as pltpu
from jax.sharding import PartitionSpec as P

kappa_leaf = 2.0
f32 = jnp.float32
i32 = jnp.int32
VMEM = pl.BlockSpec(memory_space=pltpu.VMEM)
SMEM = pl.BlockSpec(memory_space=pltpu.SMEM)
ANY = pl.BlockSpec(memory_space=pl.ANY)


def cheb_nodes():
    return np.cos((2.0 * np.arange(8) + 1.0) * np.pi / 16.0)


def lagrange_np(values):
    nodes = cheb_nodes()
    rows = []
    for center in range(8):
        weight = np.ones_like(values)
        for other in range(8):
            if other != center:
                weight = weight * (values - nodes[other]) / (nodes[center] - nodes[other])
        rows.append(weight)
    return np.stack(rows, axis=0)


def child_axis(bit):
    return 0.5 * (2 * bit - 1) + 0.5 * cheb_nodes()


def axis_maps():
    return np.stack([lagrange_np(child_axis(bit)) for bit in range(2)])


def lane_maps():
    maps = axis_maps()
    out = []
    for pick in range(4):
        both = np.kron(maps[pick // 2], maps[pick % 2])
        full = np.kron(np.eye(2), both).T
        high = full.astype(jnp.bfloat16)
        low = (full - high.astype(np.float64)).astype(jnp.bfloat16)
        out.append(np.block([[high, low], [high, np.zeros_like(low)]]))
    return np.stack(out).astype(jnp.bfloat16)


def row_maps():
    maps = axis_maps()
    rows = np.arange(8)[:, None]
    half = np.arange(128)[None, :] // 64
    k = rows // 2
    out = np.zeros((2, 8, 8, 128), np.float32)
    for bit in range(2):
        for step in range(4):
            for flip in range(2):
                to = 2 * k + half
                frm = 2 * ((k + step) % 4) + (half ^ flip)
                out[bit, 2 * step + flip] = maps[bit][to, frm]
    return out


def basis(x):
    t = cheb_nodes()[:4]
    sq = t * t
    x2 = x * x
    s = [x2 - float(v) for v in sq]
    p01 = s[0] * s[1]
    p23 = s[2] * s[3]
    rest = [s[1] * p23, s[0] * p23, p01 * s[3], p01 * s[2]]
    out = [None] * 8
    for j in range(4):
        scale = 1.0 / (np.prod([sq[j] - sq[i] for i in range(4) if i != j]) * 2.0 * t[j])
        q = rest[j] * float(scale)
        out[j] = q * (x + float(t[j]))
        out[7 - j] = q * (float(t[j]) - x)
    return out


def lanes_of(shape):
    return lax.broadcasted_iota(i32, shape, len(shape) - 1)


def lanes_of(shape):
    return lax.broadcasted_iota(i32, shape, len(shape) - 1)


CHUNKS = ((1, 3), (2, 0))
ORDER = tuple(m for chunk in CHUNKS for m in chunk)


def route(here, plan, leaf, table, labels, picked, scaled):
    bf16 = jnp.bfloat16
    cap = labels.shape[2]
    target = plan[...]
    names = leaf[...].astype(f32)
    along_x = (target - here[0]) % 4
    along_y = (target // 4 - here[1]) % 4
    first = jnp.where(here[2] == 0, along_x, along_y)
    second = jnp.where(here[2] == 0, along_y, along_x)
    place, lead, width, part_of = target * 0, target * 0, target * 0, target * 0
    for c, chunk in enumerate(CHUNKS):
        for n, m in enumerate(chunk):
            hit = second == m
            place = jnp.where(hit, ORDER.index(m), place)
            part_of = jnp.where(hit, c, part_of)
            lead = jnp.where(hit, n, lead)
            width = jnp.where(hit, len(chunk), width)
    code = place * 4 + first
    for d in range(16):
        hit = (code == d).astype(f32)
        picked[pl.ds(8 * d, 8), :] = hit
        scaled[pl.ds(8 * d, 8), :] = hit * names
    square = (128, 128)
    row, lane = rows_of(square), lanes_of(square)
    hits = picked[...].astype(bf16)
    ones = jnp.ones(square, bf16)

    def mul(a, b):
        return jnp.dot(a.astype(bf16), b.astype(bf16), preferred_element_type=f32)

    inside = mul(hits, (row < lane).astype(f32))
    ahead = mul(mul((lane < row).astype(f32), hits), ones)
    same = mul(mul(((lane < row) & (lane // 8 == row // 8)).astype(f32), hits), ones)
    order = jnp.zeros((8, 128), f32)
    slot = jnp.zeros((8, 128), f32)
    for d in range(16):
        part = slice(8 * d, 8 * d + 8)
        hit = picked[pl.ds(8 * d, 8), :]
        order = order + hit * (inside[part] + ahead[part])
        slot = slot + hit * (inside[part] + same[part])
    count = ENTRIES
    lane_w = lanes_of((1, count))
    spans = jnp.zeros((1, count), f32)
    start = jnp.zeros((1, 1), f32)
    before = jnp.zeros((1, 1), f32)
    for c in range(len(CHUNKS)):
        size = jnp.sum((part_of == c).astype(f32), keepdims=True)
        groups = jnp.floor((size + float(GROUP - 1)) * (1.0 / GROUP))
        spans = jnp.where(lane_w == 2 * c, jnp.broadcast_to(start, (1, count)), spans)
        spans = jnp.where(lane_w == 2 * c + 1, jnp.broadcast_to(groups, (1, count)), spans)
        order = order + jnp.where(
            part_of == c, jnp.broadcast_to(start - before, order.shape), 0.0
        )
        start = start + groups * float(GROUP)
        before = before + size
    goal_hi = (first * width + lead).astype(f32)
    ranks = lax.broadcasted_iota(i32, (count, 128), 0).astype(f32)
    seats = row.astype(f32)
    sub = lax.broadcasted_iota(i32, (8, 128), 0)
    lane_f = lanes_of((8, 128)).astype(f32)
    found = jnp.zeros((8, count), f32)
    marks = jnp.zeros((32, 128), f32)
    nt = (((1,), (1,)), ((), ()))
    for r in range(8):
        at = jnp.broadcast_to(order[r : r + 1, :], (count, 128)) == ranks
        goal = jnp.broadcast_to(goal_hi[r : r + 1, :], (8, 128))
        seat = jnp.broadcast_to(slot[r : r + 1, :], (8, 128))
        values = jnp.where(
            sub == 0, 2.0 * lane_f - (lanes_of((8, 128)) % 8).astype(f32),
            jnp.where(sub == 1, float(r), jnp.where(sub == 2, goal, jnp.where(sub == 3, seat, 1.0))),
        )
        found = found + lax.dot_general(
            values.astype(bf16), at.astype(f32).astype(bf16), nt, preferred_element_type=f32
        )
        both = jnp.concatenate(
            [scaled[pl.ds(r, 16, stride=8), :], picked[pl.ds(r, 16, stride=8), :]], axis=0
        )
        sits = jnp.broadcast_to(slot[r : r + 1, :], square) == seats
        marks = marks + lax.dot_general(
            both.astype(bf16), sits.astype(f32).astype(bf16), nt, preferred_element_type=f32
        )
    lines = (found[0:1] + found[1:2] * 256.0).astype(i32)
    goals = (found[2:3] * float(cap_rows(cap)) + found[3:4] + found[4:5]).astype(i32)
    for n, values in enumerate((lines, goals)):
        for r in range(count // 128):
            at = n * (count // 128) + r
            table[at : at + 1, :] = values[:, 128 * r : 128 * r + 128]
    at = 2 * (count // 128)
    table[at : at + 1, :] = spans[:, :128].astype(i32)
    label = marks[:16] + 256.0 * (1.0 - marks[16:])
    for d in range(16):
        total = jnp.sum(marks[16 + d : 17 + d], axis=1, keepdims=True)
        labels[d] = jnp.where(
            sub == 0,
            jnp.broadcast_to(label[d : d + 1], (8, 128)),
            jnp.broadcast_to(total, (8, 128)),
        )


def cap_rows(cap):
    return cap + 1


GROUP = 16
ENTRIES = 1152


def expand_kernel(chunk, *refs):
    if chunk:
        table, labels, pts, *refs = refs
    else:
        here, plan, leaf, pts, *refs = refs
    outs, refs = refs[:4], refs[4:]
    if not chunk:
        listed, labels, *refs = refs
    held, all_pts, stage, bx, by, bz, sems, load_sems, *refs = refs
    first = sum(len(c) for c in CHUNKS[:chunk])
    wide = len(CHUNKS[chunk])
    rows = outs[0].shape[1]
    cap = rows - 1
    span = all_pts.shape[0] // 5
    loads = [
        pltpu.make_async_copy(
            pts.at[pl.ds(span * axis, span)], all_pts.at[pl.ds(span * axis, span)],
            load_sems.at[axis],
        )
        for axis in range(5)
    ]
    for load in loads:
        load.start()
    if not chunk:
        table, picked, scaled, sem = refs
        route(here, plan, leaf, listed, labels, picked, scaled)
        copy = pltpu.make_async_copy(listed, table, sem)
        copy.start()
        copy.wait()

    def look(base, which, u=0):
        if chunk:
            return table[base + (which * ENTRIES + u)]
        return table[(base >> 7) + which * (ENTRIES // 128), (base & 127) + u]

    for k in range(4):
        for n in range(wide):
            held[1 + (k * wide + n) * rows + cap] = labels[4 * (first + n) + k]
    begin = look(i32(0), 2, 2 * chunk)
    trips = look(i32(0), 2, 2 * chunk + 1)
    for load in loads:
        load.wait()

    def fetch(g, u, bank):
        line = look(begin + g * GROUP, 0, u)
        for axis in range(3):
            for h in range(2):
                stage[bank, axis, h, pl.ds(u, 1), :] = all_pts[
                    pl.ds(line + (span * axis + 8 * h), 1), :
                ]

    def tabulate(piece, bank):
        u, h, axis = 8 * (piece // 6), piece // 3 % 2, piece % 3
        values = basis(stage[bank, axis, h, pl.ds(u, 8), :])
        for a in range(8):
            if axis == 1:
                by[bank, h, pl.ds(GROUP * a + u, 8), :] = values[a]
            else:
                ref = bz if axis else bx
                ref[bank, h, pl.ds(8 * u + a, 8, stride=8), :] = values[a]

    def consume(g, u, bank):
        base = begin + g * GROUP
        line = look(base, 0, u)
        weighted, pair = [], []
        for h in range(2):
            lx = bx[bank, h, pl.ds(8 * u, 8), :]
            lz = bz[bank, h, pl.ds(8 * u, 8), :]
            re, im = (
                jnp.broadcast_to(
                    all_pts[pl.ds(line + (span * (3 + part) + 8 * h), 1), :], lx.shape
                )
                for part in range(2)
            )
            weighted.append(jnp.concatenate([re * lx, im * lx], axis=0).astype(jnp.bfloat16))
            pair.append(
                jnp.concatenate(
                    [
                        jnp.broadcast_to(by[bank, h, pl.ds(GROUP * b + u, 1), :], lz.shape) * lz
                        for b in range(8)
                    ],
                    axis=0,
                ).astype(jnp.bfloat16)
            )
        res = lax.dot_general(
            jnp.concatenate(weighted, axis=1),
            jnp.concatenate(pair, axis=1),
            (((1,), (1,)), ((), ())),
            preferred_element_type=f32,
        )
        held[look(base, 1, u)] = jnp.concatenate([res[:8], res[8:]], axis=1)

    pieces = 6 * GROUP // 8
    for u in range(GROUP):
        fetch(0, u, 0)
    for piece in range(pieces):
        tabulate(piece, 0)
    for u in range(GROUP):
        fetch(1, u, 1)

    def step(g, carry):
        bank = g & 1
        for u in range(GROUP):
            consume(g, u, bank)
            if u % 4 == 3:
                for piece in range(3 * (u // 4), 3 * (u // 4) + 3):
                    tabulate(piece, 1 - bank)
                for v in range(u - 3, u + 1):
                    fetch(g + 2, v, bank)
        return carry

    lax.fori_loop(0, trips, step, 0)
    copies = []
    for k in range(4):
        for n in range(wide):
            copies.append(
                pltpu.make_async_copy(
                    held.at[pl.ds(1 + (k * wide + n) * rows, rows)], outs[k].at[n], sems.at[k, n]
                )
            )
    for copy in copies:
        copy.start()
    for copy in copies:
        copy.wait()


def expand(chunk, routing, pts, cap):
    wide = len(CHUNKS[chunk])
    out_shape = [jax.ShapeDtypeStruct((wide, cap + 1, 8, 128), f32)] * 4
    out_specs = [ANY] * 4
    scratch = []
    if chunk:
        in_specs = [SMEM, VMEM, ANY]
    else:
        in_specs = [SMEM, VMEM, VMEM, ANY]
        out_shape += [
            jax.ShapeDtypeStruct((24, 128), i32),
            jax.ShapeDtypeStruct((16, 8, 128), f32),
        ]
        out_specs += [VMEM] * 2
        scratch = [
            pltpu.SMEM((24, 128), i32),
            pltpu.VMEM((128, 128), f32),
            pltpu.VMEM((128, 128), f32),
            pltpu.SemaphoreType.DMA(()),
        ]
    return pl.pallas_call(
        functools.partial(expand_kernel, chunk),
        out_shape=out_shape,
        in_specs=in_specs,
        out_specs=out_specs,
        scratch_shapes=[
            pltpu.VMEM((4 * wide * (cap + 1) + 1, 8, 128), f32),
            pltpu.VMEM(pts.shape, f32),
            pltpu.VMEM((2, 3, 2, GROUP, 128), f32),
            *[pltpu.VMEM((2, 2, 8 * GROUP, 128), f32)] * 3,
            pltpu.SemaphoreType.DMA((4, wide)),
            pltpu.SemaphoreType.DMA((5,)),
            *scratch,
        ],
        cost_estimate=pl.CostEstimate(
            flops=wide * (1 << 28), bytes_accessed=1 << 23, transcendentals=0
        ),
        name="expand",
    )(*routing, pts)


def gather_kernel(wide, *refs):
    arrived, outs = refs[:4], refs[4 : 4 + wide]
    held, banks, labels, names, sem, sems = refs[4 + wide :]
    cap = held.shape[2] - 1
    loads = [pltpu.make_async_copy(arrived[k], held.at[k], sems.at[k]) for k in range(4)]
    for load in loads:
        load.start()
    for n in range(wide):
        outs[n][...] = jnp.zeros(outs[n].shape, f32)
        for bank in range(3):
            banks[bank, n] = jnp.zeros(outs[n].shape, f32)
    for load in loads:
        load.wait()
    for k in range(4):
        for n in range(wide):
            labels[pl.ds(8 * (k * wide + n), 8), :] = held[k, n, cap].astype(i32)
    copy = pltpu.make_async_copy(labels, names, sem)
    copy.start()
    copy.wait()
    for k in range(4):
        most = names[8 * k * wide + 1, 0]
        for n in range(1, wide):
            most = jnp.maximum(most, names[8 * (k * wide + n) + 1, 0])

        def rows4(r, carry):
            for u in range(4):
                for n in range(wide):
                    slot = r * 4 + u
                    where = names[8 * (k * wide + n), slot]
                    if u:
                        banks[u - 1, n, where] = banks[u - 1, n, where] + held[k, n, slot]
                    else:
                        outs[n][where] = outs[n][where] + held[k, n, slot]
            return carry

        lax.fori_loop(0, (most + 3) // 4, rows4, 0)

    def join(i, carry):
        part = pl.ds(pl.multiple_of(i * 16, 16), 16)
        for n in range(wide):
            outs[n][part] = (outs[n][part] + banks[0, n, part]) + (
                banks[1, n, part] + banks[2, n, part]
            )
        return carry

    lax.fori_loop(0, (outs[0].shape[0] - 1) // 16, join, 0)


def gather(arrived, leaf_count):
    wide, rows = arrived[0].shape[:2]
    return pl.pallas_call(
        functools.partial(gather_kernel, wide),
        out_shape=[jax.ShapeDtypeStruct((leaf_count + 1, 8, 128), f32)] * wide,
        in_specs=[pl.BlockSpec(memory_space=pl.ANY)] * 4,
        out_specs=[VMEM] * wide,
        scratch_shapes=[
            pltpu.VMEM((4, wide, rows, 8, 128), f32),
            pltpu.VMEM((3, wide, leaf_count + 1, 8, 128), f32),
            pltpu.VMEM((32 * wide, 128), i32),
            pltpu.SMEM((32 * wide, 128), i32),
            pltpu.SemaphoreType.DMA(()),
            pltpu.SemaphoreType.DMA((4,)),
        ],
        cost_estimate=pl.CostEstimate(
            flops=wide * (1 << 26), bytes_accessed=wide << 22, transcendentals=0
        ),
        compiler_params=pltpu.CompilerParams(vmem_limit_bytes=(8 + 10 * wide) << 20),
        name="gather",
    )(*arrived)


def rows_of(shape):
    return lax.broadcasted_iota(i32, shape, len(shape) - 2)


def swap_rows(t):
    even = rows_of(t.shape) % 2 == 0
    axis = len(t.shape) - 2
    return jnp.where(even, pltpu.roll(t, 7, axis), pltpu.roll(t, 1, axis))


def spin(t, cosine, sine):
    return t * cosine + swap_rows(t) * sine


def row_mix(t, maps, bit):
    flipped = pltpu.roll(t, 64, 2)
    total = None
    for step in range(4):
        for flip in range(2):
            part = flipped if flip else t
            if step:
                part = pltpu.roll(part, 8 - 2 * step, 1)
            term = part * maps[bit, 2 * step + flip]
            total = term if total is None else total + term
    return total


SEATS = 36


def turn(ca, sa, cb, sb):
    return ca * cb - sa * sb, sa * cb + ca * sb


def twice(c, s):
    return c * c - s * s, 2.0 * (s * c)


def phases_kernel(
    here, slots, boxes, cones, box_cones, cosine, sine, p0c, p0s, p1c, p1s, ec, es, goal,
    t0c, t0s, t1c, t1s, t2c, t2s,
):
    side = here[2]
    sign = jnp.where(rows_of((8, 128)) % 2 == 0, -1.0, 1.0)

    def cone_tables(n, carry):
        xs = [(cosine[n, v], sine[n, v]) for v in range(3)]
        wide = [
            tuple(jnp.broadcast_to(t[n, 3, pl.ds(v, 1), :], (8, 128)) for t in (cosine, sine))
            for v in range(5)
        ]
        t1c[n], t1s[n] = turn(*xs[2], *wide[4])
        xs2 = [twice(*x) for x in xs[:2]]
        for v in range(4):
            wide2 = twice(*wide[v])
            for bit in range(2):
                at = n * 8 + 4 * bit + v
                t0c[at], t0s[at] = turn(*xs[bit], *wide[v])
                t2c[at], t2s[at] = turn(*xs2[bit], *wide2)
        return carry

    lax.fori_loop(0, cosine.shape[0], cone_tables, 0)

    def child(j, carry):
        for o in range(8):
            p = slots[32 * o + j]
            e = cones[p] * 8 + o
            p0c[o, j] = t0c[e]
            p0s[o, j] = t0s[e] * sign
            owner = p >> 5
            goal[32 * o + j] = ((((owner & 1) ^ side) << 2) + (owner >> 1)) * SEATS + (p & 31)
            a = cones[8 * j + o]
            b = box_cones[boxes[32 * o + j]] * 8 + o
            c, s = turn(t1c[a], t1s[a], t2c[b], t2s[b])
            p1c[o, j] = c
            p1s[o, j] = s * sign
        return carry

    lax.fori_loop(0, 32, child, 0)
    me = 2 * here[3] + side
    for n in range(SEATS):
        if n < 32:
            a = cones[32 * me + n]
            c, s = t1c[a], t1s[a]
        else:
            a = box_cones[4 * me + n - 32]
            c, s = twice(t1c[a], t1s[a])
        ec[n] = c
        es[n] = s * sign


def lane_mix(t, both, octant):
    count = t.shape[0]
    flat = t.reshape(count * 8, 128)
    high = flat.astype(jnp.bfloat16)
    low = (flat - high.astype(f32)).astype(jnp.bfloat16)
    res = jnp.dot(
        jnp.concatenate([high, low], axis=1), both[octant % 4], preferred_element_type=f32
    )
    return (res[:, :128] + res[:, 128:]).reshape(count, 8, 128)


def levels_kernel(
    here, goal, boxes, a0, a1, a2, a3, p0c, p0s, p1c, p1s, both, rows, leaves, mine, other,
    held, turns, lanes_in, rows_in, solved, acc, upper, moved, sems, out_sems,
):
    count = leaves.shape[0]
    sums = [
        pltpu.make_async_copy(ref.at[pl.ds(0, count)], held.at[n], sems.at[n])
        for n, ref in enumerate((a0, a1, a2, a3))
    ]
    maps = [
        pltpu.make_async_copy(both, lanes_in, sems.at[4]),
        pltpu.make_async_copy(rows, rows_in, sems.at[5]),
    ]
    angles = [
        pltpu.make_async_copy(ref, turns.at[n], sems.at[6 + n])
        for n, ref in enumerate((p0c, p0s, p1c, p1s))
    ]
    for copy in sums + maps + angles:
        copy.start()
    acc[...] = jnp.zeros(acc.shape, f32)
    upper[...] = jnp.zeros(upper.shape, f32)
    for copy in sums:
        copy.wait()
    step = 16
    shape = (step, 8, 128)
    own = rows_of(shape) % 2 == lanes_of(shape) // 64

    def settle(n, carry):
        base = pl.multiple_of(n * step, step)
        t = (held[0, pl.ds(base, step)] + held[1, pl.ds(base, step)]) + (
            held[2, pl.ds(base, step)] + held[3, pl.ds(base, step)]
        )
        solved[pl.ds(base, step)] = jnp.where(own, t, swap_rows(pltpu.roll(t, 64, 2)))
        return carry

    lax.fori_loop(0, count // step, settle, 0)
    done = [pltpu.make_async_copy(solved, leaves, out_sems.at[8])]
    done[0].start()
    for copy in maps + angles[:2]:
        copy.wait()

    def spread(o, start, ref, spots):
        sums = [ref[spots[j]] + moved[o % 2, start + j] for j in range(8)]
        for j in range(8):
            ref[spots[j]] = sums[j]

    for o in range(8):
        for part in range(0, 32, 8):
            t = jnp.stack([solved[8 * (part + j) + o] for j in range(8)])
            t = spin(t, turns[0, o, part : part + 8], turns[1, o, part : part + 8])
            moved[o % 2, part : part + 8] = row_mix(lane_mix(t, lanes_in, o), rows_in, o // 4)
        for part in range(0, 32, 8):
            spread(o, part, acc, [goal[32 * o + part + j] for j in range(8)])

    apart = [here[2] * 4 * SEATS, (1 - here[2]) * 4 * SEATS]
    for copy in angles[2:]:
        copy.wait()
    for o in range(8):
        for part in range(0, 32, 8):
            tiles = []
            for j in range(8):
                p = 8 * (part + j) + o
                owner = p // 32
                tiles.append(acc[(owner // 2) * SEATS + p % 32 + apart[owner % 2]])
            t = spin(
                jnp.stack(tiles), turns[2, o, part : part + 8], turns[3, o, part : part + 8]
            )
            moved[o % 2, part : part + 8] = lane_mix(t, lanes_in, o)
        for part in range(0, 32, 8):
            spread(
                o, part, upper,
                [boxes[32 * o + part + j] + 32 * (o // 4) for j in range(8)],
            )
    for part in range(0, 32, 8):
        t = row_mix(upper[part : part + 8], rows_in, 0)
        t = t + row_mix(upper[32 + part : 40 + part], rows_in, 1)
        for j in range(8):
            q = part + j
            owner = q // 4
            acc[(owner // 2) * SEATS + 32 + q % 4 + apart[owner % 2]] = t[j]
    for k in range(4):
        z = (here[3] + k) % 4
        done += [
            pltpu.make_async_copy(
                acc.at[pl.ds((4 + z) * SEATS, SEATS)], other.at[k], out_sems.at[4 + k]
            ),
            pltpu.make_async_copy(acc.at[pl.ds(z * SEATS, SEATS)], mine.at[k], out_sems.at[k]),
        ]
    for copy in done[1:]:
        copy.start()
    for copy in done:
        copy.wait()


def close_kernel(g0, g1, g2, g3, ec, es, out_one, out_two):
    owned = out_one.shape[0]
    for n in range(SEATS):
        t = spin((g0[n] + g1[n]) + (g2[n] + g3[n]), ec[n], es[n])
        if n < owned:
            out_one[n] = t
        else:
            out_two[n - owned] = t


def cone_places():
    nodes = cheb_nodes()
    rows = np.arange(8)[:, None]
    lanes = np.arange(128)[None, :]
    a = 2 * (rows // 2) + lanes // 64
    out = np.zeros((3, 4, 8, 128))
    out[0, 0], out[0, 1], out[0, 2] = child_axis(0)[a], child_axis(1)[a], -nodes[a]
    b, c = np.arange(128) % 64 // 8, np.arange(128) % 8
    for v in range(4):
        out[1, 3, v], out[2, 3, v] = child_axis(v // 2)[b], child_axis(v % 2)[c]
    out[1, 3, 4], out[2, 3, 4] = -nodes[b], -nodes[c]
    return out.astype(np.float32)


def to_nodes(tiles):
    count = tiles.shape[0]
    return tiles.reshape(count, 4, 2, 128).transpose(0, 2, 1, 3).reshape(count, 2, 512)


def cone_vectors(cone_angles):
    azimuth = cone_angles[:, 0]
    polar = cone_angles[:, 1]
    return jnp.stack(
        [jnp.cos(azimuth) * jnp.sin(polar), jnp.sin(azimuth) * jnp.sin(polar), jnp.cos(polar)],
        axis=1,
    )


def hop(x, shift, leg, groups):
    pairs = []
    for s in range(16):
        for g in range(groups):
            y, x0 = s // 4, s % 4
            if g % 2 == leg:
                x0 = (x0 + shift) % 4
            else:
                y = (y + shift) % 4
            pairs.append((s * groups + g, (4 * y + x0) * groups + g))
    return lax.ppermute(x, ("sfc", "grp"), pairs)


def around(x, shift, groups):
    pairs = [(g, (g + 2 * shift) % groups) for g in range(groups)]
    return lax.ppermute(x, "grp", pairs)


def after(value, *others):
    return lax.optimization_barrier((value, *others))[0]


def per_device(
    bin_points, bin_plan, bin_leaf, leaf_slots, box_slots, parent_cone, box_cone, cone_angles
):
    groups = lax.axis_size("grp")
    rank = lax.axis_index("grp")
    cap = bin_points.shape[0] // 8
    leaf_count = leaf_slots.shape[2] * 8
    first_owned = parent_cone.shape[1] // groups
    second_owned = box_cone.shape[1] // groups
    tile = jax.ShapeDtypeStruct((8, 128), f32)

    def tiles(*lead):
        return jax.ShapeDtypeStruct((*lead, *tile.shape), f32)

    me = lax.axis_index("sfc")
    here = jnp.stack([me % 4, me // 4, rank % 2, rank // 2]).astype(i32)
    bins, _, width = bin_points.shape
    pts = jnp.transpose(bin_points.reshape(bins // 8, 8, 5, width // 128, 128), (2, 0, 3, 1, 4))
    pts = pts.reshape(-1, 128)
    arrived = []
    routing = (here, bin_plan.reshape(bins // 128, 128), bin_leaf.reshape(bins // 128, 128))
    for c in range(len(CHUNKS)):
        sent = expand(c, routing, pts, cap)
        if not c:
            *sent, table, labels = sent
            table = table.reshape(-1)
        table = after(table, sent[0])
        routing = (table, labels)
        moved = [sent[0]]
        for k in (2, 1, 3):
            moved.append(hop(sent[k], k, 0, groups))
        arrived.append(moved)

    cone_angles = after(cone_angles, sent[0])
    directions = cone_vectors(cone_angles)
    places = jnp.asarray(cone_places())
    angle = (
        directions[:, 0, None, None, None] * places[None, 0]
        + directions[:, 1, None, None, None] * places[None, 1]
        + directions[:, 2, None, None, None] * places[None, 2]
    ) * kappa_leaf
    make_phases = pl.pallas_call(
        phases_kernel,
        out_shape=(tiles(8, 32),) * 4 + (tiles(SEATS),) * 2 + (jax.ShapeDtypeStruct((256,), i32),),
        in_specs=[SMEM] * 5 + [VMEM] * 2,
        out_specs=(VMEM,) * 6 + (SMEM,),
        scratch_shapes=[pltpu.VMEM((n, 8, 128), f32) for n in (128, 128, 16, 16, 128, 128)],
        compiler_params=pltpu.CompilerParams(vmem_limit_bytes=16 << 20),
        name="phases",
    )
    slots, boxes = leaf_slots.reshape(-1), box_slots.reshape(-1)
    p0c, p0s, p1c, p1s, ec, es, goal = make_phases(
        here, slots, boxes, parent_cone[0], box_cone[0], jnp.cos(angle), jnp.sin(angle)
    )

    held = [None] * 4
    last = sent[0]
    for c, chunk in enumerate(CHUNKS):
        got = [after(arrived[c][0], last)] + arrived[c][1:]
        sums = gather(got, leaf_count)
        last = sums[0]
        for m, part in zip(chunk, sums):
            held[m] = hop(part, m, 1, groups) if m else part

    leaves, mine, other = pl.pallas_call(
        levels_kernel,
        out_shape=(tiles(leaf_count), tiles(4, SEATS), tiles(4, SEATS)),
        in_specs=[SMEM] * 3 + [ANY] * 10,
        out_specs=(ANY,) * 3,
        scratch_shapes=[
            pltpu.VMEM((4, leaf_count, 8, 128), f32),
            pltpu.VMEM((4, 8, 32, 8, 128), f32),
            pltpu.VMEM((4, 256, 256), jnp.bfloat16),
            pltpu.VMEM((2, 8, 8, 128), f32),
            pltpu.VMEM((leaf_count, 8, 128), f32),
            pltpu.VMEM((8 * SEATS, 8, 128), f32),
            pltpu.VMEM((64, 8, 128), f32),
            pltpu.VMEM((2, 32, 8, 128), f32),
            pltpu.SemaphoreType.DMA((10,)),
            pltpu.SemaphoreType.DMA((9,)),
        ],
        compiler_params=pltpu.CompilerParams(vmem_limit_bytes=20 << 20),
        name="levels",
    )(
        here, goal, boxes, *held, p0c, p0s, p1c, p1s,
        jnp.asarray(lane_maps()), jnp.asarray(row_maps()),
    )
    swapped = lax.ppermute(other, "grp", [(g, g ^ 1) for g in range(groups)])
    blocks = [mine[k] + swapped[k] for k in range(4)]
    got = [blocks[0]] + [around(blocks[k], k, groups) for k in (1, 2, 3)]
    one, two = pl.pallas_call(
        close_kernel,
        out_shape=(tiles(first_owned), tiles(second_owned)),
        in_specs=[VMEM] * 6,
        out_specs=(VMEM, VMEM),
        compiler_params=pltpu.CompilerParams(vmem_limit_bytes=8 << 20),
        name="close",
    )(*got, ec, es)
    return (to_nodes(leaves), to_nodes(one), to_nodes(two))


def solution(mesh):
    placed = (
        P(("sfc", "grp"), None, None),
        P(("sfc", "grp"), None),
        P(("sfc", "grp")),
        P("sfc", None, "grp"),
        P("sfc", None, None),
        P("sfc", None),
        P("sfc", None),
        P(),
    )

    return jax.shard_map(
        per_device,
        mesh=mesh,
        in_specs=placed,
        out_specs=(
            P(("sfc", "grp"), None, None),
            P(("sfc", "grp"), None, None),
            P(("sfc", "grp"), None, None),
        ),
        check_vma=False,
    )
```

profile of v0, /device:TPU:0, one launch (start us, length us, event | category | flops | bytes accessed | tf_op | source)
XLA Modules:
  0.0 133.2 jit_solution(16882564546990975858)
XLA Ops:
  0.7 0.7 pad_add_fusion.refs_0_.here
  1.3 22.8 %expand.2 = (f32[2,129,8,128]{3,2,1,0:T(8,128)}, f32[2,129,8,128]{3,2,1,0:T(8,128)}, f32[2,129,8,128]{3,2,1,0:T(8,128)}, f32[2,129,8,128]{3,2,1,0:T(8,128)}, s32[24,128]{1,0:T(8,128)}, /*index=5*/f32[16,8,128]{2,1,0:T(8,128)}) custom-call(s32[4]{0:T(128)} %pad_add_fusion.refs_0_.here, s32[8,128]{1,0:T(8,128)} %bitcast.48, s32[8,128]{1,0:T(8,128)} %bitcast.49, ...), custom_call_target="tpu_custom_call" | custom-call | flops 536870912 | bytes 8388608 | tf_op jit(solution)/shard_map/expand/pallas_call | solution.py:352
  24.2 2.4 %collective-permute-start = (f32[2,129,8,128]{3,2,1,0:T(8,128)}, f32[2,129,8,128]{3,2,1,0:T(8,128)S(1)}, u32[]{:S(2)}, u32[]{:S(2)}) collective-permute-start(f32[2,129,8,128]{3,2,1,0:T(8,128)} %get-tuple-element.41), channel_id=1, source_target_pairs={{0,16},{1,65},{2,18},{3,67},{4,20},{5,69},{6,22},{7,71},{8,24},{9,... | collective-permute-start | bytes 3170312 | tf_op jit(solution)/shard_map/ppermute | solution.py:688
  26.5 1.9 %collective-permute-start.1 = (f32[2,129,8,128]{3,2,1,0:T(8,128)}, f32[2,129,8,128]{3,2,1,0:T(8,128)S(1)}, u32[]{:S(2)}, u32[]{:S(2)}) collective-permute-start(f32[2,129,8,128]{3,2,1,0:T(8,128)} %get-tuple-element.42), channel_id=1, source_target_pairs={{0,8},{1,33},{2,10},{3,35},{4,12},{5,37},{6,14},{7,39},{8,16},{9,4... | collective-permute-start | bytes 3170312 | tf_op jit(solution)/shard_map/ppermute | solution.py:688
  28.4 1.4 %collective-permute-start.2 = (f32[2,129,8,128]{3,2,1,0:T(8,128)}, f32[2,129,8,128]{3,2,1,0:T(8,128)}, u32[]{:S(2)}, u32[]{:S(2)}) collective-permute-start(f32[2,129,8,128]{3,2,1,0:T(8,128)} %get-tuple-element.43), channel_id=1, source_target_pairs={{0,24},{1,97},{2,26},{3,99},{4,28},{5,101},{6,30},{7,103},{8,0},{9... | collective-permute-start | bytes 3170312 | tf_op jit(solution)/shard_map/ppermute | solution.py:688
  29.8 16.4 %expand.3 = (f32[2,129,8,128]{3,2,1,0:T(8,128)}, f32[2,129,8,128]{3,2,1,0:T(8,128)}, f32[2,129,8,128]{3,2,1,0:T(8,128)}, f32[2,129,8,128]{3,2,1,0:T(8,128)}) custom-call(s32[3072]{0:T(1024)} %bitcast.47, f32[16,8,128]{2,1,0:T(8,128)} %get-tuple-element.36.refs_1_, f32[10240,128]{1,0:T(8,128)} %bitcast.46), custom_call_target="tpu_custom_call" | custom-call | flops 536870912 | bytes 8388608 | tf_op jit(solution)/shard_map/expand/pallas_call | solution.py:352
  46.2 1.6 %collective-permute-start.3 = (f32[2,129,8,128]{3,2,1,0:T(8,128)}, f32[2,129,8,128]{3,2,1,0:T(8,128)S(1)}, u32[]{:S(2)}, u32[]{:S(2)}) collective-permute-start(f32[2,129,8,128]{3,2,1,0:T(8,128)} %get-tuple-element.46), channel_id=1, source_target_pairs={{0,16},{1,65},{2,18},{3,67},{4,20},{5,69},{6,22},{7,71},{8,24},{9,... | collective-permute-start | bytes 3170312 | tf_op jit(solution)/shard_map/ppermute | solution.py:688
  47.8 0.1 collective-permute-start.4
  48.0 0.0 collective-permute-done.refs_1_
  48.0 3.1 %collective-permute-start.5 = (f32[2,129,8,128]{3,2,1,0:T(8,128)}, f32[2,129,8,128]{3,2,1,0:T(8,128)S(1)}, u32[]{:S(2)}, u32[]{:S(2)}) collective-permute-start(f32[2,129,8,128]{3,2,1,0:T(8,128)} %get-tuple-element.48), channel_id=1, source_target_pairs={{0,24},{1,97},{2,26},{3,99},{4,28},{5,101},{6,30},{7,103},{8,0},{9... | collective-permute-start | bytes 3170312 | tf_op jit(solution)/shard_map/ppermute | solution.py:688
  51.1 1.1 collective-permute-done.1.refs_2_
  52.2 0.8 collective-permute-done.2.refs_3_
  53.0 7.8 %gather.2 = (f32[257,8,128]{2,1,0:T(8,128)}, f32[257,8,128]{2,1,0:T(8,128)}) custom-call(f32[2,129,8,128]{3,2,1,0:T(8,128)S(1)} %copy-done.1, f32[2,129,8,128]{3,2,1,0:T(8,128)S(1)} %collective-permute-done.refs_1_, f32[2,129,8,128]{3,2,1,0:T(8,128)S(1)} %collective-permute-done.1.refs_2_, f32[2,129,8,128]{3,2,1,0:T(8,128)} %collective-permute-done.2.refs_3_), custom_call_target="tpu_custom_call" | custom-call | flops 134217728 | bytes 8388608 | tf_op jit(solution)/shard_map/gather/pallas_call | solution.py:423
  60.8 0.1 collective-permute-start.6
  60.9 0.0 copy-start.10
  60.9 0.0 copy-start.11
  60.9 0.0 copy-start.12
  60.9 0.0 copy-start.7
  60.9 0.0 copy-start.8
  60.9 0.0 copy-start.9
  60.9 0.0 copy-start.5
  61.0 0.0 copy-start.6
  61.0 3.3 %collective-permute-start.8 = (f32[257,8,128]{2,1,0:T(8,128)}, f32[257,8,128]{2,1,0:T(8,128)S(1)}, u32[]{:S(2)}, u32[]{:S(2)}) collective-permute-start(f32[257,8,128]{2,1,0:T(8,128)} %get-tuple-element.51), channel_id=1, source_target_pairs={{0,96},{1,25},{2,98},{3,27},{4,100},{5,29},{6,102},{7,31},{8,104},... | collective-permute-start | bytes 3158024 | tf_op jit(solution)/shard_map/ppermute | solution.py:688
  64.2 1.7 %collective-permute-done.3.refs_1_ = f32[2,129,8,128]{3,2,1,0:T(8,128)S(1)} collective-permute-done((f32[2,129,8,128]{3,2,1,0:T(8,128)}, f32[2,129,8,128]{3,2,1,0:T(8,128)S(1)}, u32[]{:S(2)}, u32[]{:S(2)}) %collective-permute-start.3) | collective-permute-done | bytes 1056800 | tf_op jit(solution)/shard_map/ppermute | solution.py:688
  65.9 20.2 %collective-permute-done.4.refs_2_ = f32[2,129,8,128]{3,2,1,0:T(8,128)S(1)} collective-permute-done((f32[2,129,8,128]{3,2,1,0:T(8,128)}, f32[2,129,8,128]{3,2,1,0:T(8,128)S(1)}, u32[]{:S(2)}, u32[]{:S(2)}) %collective-permute-start.4) | collective-permute-done | bytes 1056800 | tf_op jit(solution)/shard_map/ppermute | solution.py:688
  86.1 0.7 collective-permute-done.5.refs_3_
  86.8 5.2 %gather.3 = (f32[257,8,128]{2,1,0:T(8,128)}, f32[257,8,128]{2,1,0:T(8,128)S(1)}) custom-call(f32[2,129,8,128]{3,2,1,0:T(8,128)S(1)} %copy-done, f32[2,129,8,128]{3,2,1,0:T(8,128)S(1)} %collective-permute-done.3.refs_1_, f32[2,129,8,128]{3,2,1,0:T(8,128)S(1)} %collective-permute-done.4.refs_2_, f32[2,129,8,128]{3,2,1,0:T(8,128)S(1)} %collective-permute-done.5.refs_3_), custom_call_target="tpu_custom_call" | custom-call | flops 134217728 | bytes 8388608 | tf_op jit(solution)/shard_map/gather/pallas_call | solution.py:423
  92.0 0.0 copy-start.3
  92.0 3.1 %collective-permute-start.7 = (f32[257,8,128]{2,1,0:T(8,128)}, f32[257,8,128]{2,1,0:T(8,128)}, u32[]{:S(2)}, u32[]{:S(2)}) collective-permute-start(f32[257,8,128]{2,1,0:T(8,128)} %get-tuple-element.50), channel_id=1, source_target_pairs={{0,64},{1,17},{2,66},{3,19},{4,68},{5,21},{6,70},{7,23},{8,72},{9,... | collective-permute-start | bytes 3158024 | tf_op jit(solution)/shard_map/ppermute | solution.py:688
  95.1 0.1 reshape.81.boxes
  95.2 0.1 reshape.80.slots
  95.3 0.1 multiply_bitcast_fusion.1
  95.4 1.1 fusion
  96.5 3.8 %phases.1 = (f32[8,32,8,128]{3,2,1,0:T(8,128)S(1)}, f32[8,32,8,128]{3,2,1,0:T(8,128)S(1)}, f32[8,32,8,128]{3,2,1,0:T(8,128)S(1)}, f32[8,32,8,128]{3,2,1,0:T(8,12...) custom-call(s32[4]{0:T(128)S(1)} %copy-done.4, s32[256]{0:T(256)S(1)} %reshape.80.slots, ...), custom_call_target="tpu_custom_call" | custom-call | tf_op jit(solution)/shard_map/phases/pallas_call | solution.py:751
  100.2 0.0 collective-permute-done.8.a3
  100.3 0.0 collective-permute-done.6.a1
  100.3 8.5 %collective-permute-done.7.a2 = f32[257,8,128]{2,1,0:T(8,128)} collective-permute-done((f32[257,8,128]{2,1,0:T(8,128)}, f32[257,8,128]{2,1,0:T(8,128)}, u32[]{:S(2)}, u32[]{:S(2)}) %collective-permute-start.7) | collective-permute-done | bytes 1052704 | tf_op jit(solution)/shard_map/ppermute | solution.py:688
  108.7 7.6 %levels.1 = (f32[256,8,128]{2,1,0:T(8,128)}, f32[4,36,8,128]{3,2,1,0:T(8,128)S(1)}, f32[4,36,8,128]{3,2,1,0:T(8,128)S(1)}) custom-call(s32[4]{0:T(128)S(1)} %copy-done.4, s32[256]{0:T(256)S(1)} %get-tuple-element.39.goal, s32[256]{0:T(256)S(1)} %reshape.81.boxes, f32[257,8,128]{2,1,0:T(8,128)S(1)} %get-tuple-element.49.a0, ...), custom_call_target="tpu_custom_call" | custom-call | tf_op jit(solution)/shard_map/levels/pallas_call | solution.py:764
  116.3 0.1 collective-permute-start.9
  116.4 2.0 %collective-permute-done.9 = f32[4,36,8,128]{3,2,1,0:T(8,128)S(1)} collective-permute-done((f32[4,36,8,128]{3,2,1,0:T(8,128)S(1)}, f32[4,36,8,128]{3,2,1,0:T(8,128)S(1)}, u32[]{:S(2)}, u32[]{:S(2)}) %collective-permute-start.9) | collective-permute-done | bytes 589856 | tf_op jit(solution)/shard_map/ppermute | solution.py:787
  118.4 0.1 fusion.2
  118.5 3.8 %collective-permute-start.12 = (f32[36,8,128]{2,1,0:T(8,128)S(1)}, f32[36,8,128]{2,1,0:T(8,128)S(1)}, u32[]{:S(2)}, u32[]{:S(2)}) collective-permute-start(f32[36,8,128]{2,1,0:T(8,128)S(1)} %get-tuple-element.63), channel_id=1, source_target_pairs={{0,6},{1,7},{2,0},{3,1},{4,2},{5,3},{6,4},{7,5},{8,14},{9,15},{10,... | collective-permute-start | bytes 442376 | tf_op jit(solution)/shard_map/ppermute | solution.py:693
  122.2 1.2 collective-permute-start.11
  123.5 0.3 collective-permute-start.10
  123.8 5.1 %collective-permute-done.12.g3 = f32[36,8,128]{2,1,0:T(8,128)S(1)} collective-permute-done((f32[36,8,128]{2,1,0:T(8,128)S(1)}, f32[36,8,128]{2,1,0:T(8,128)S(1)}, u32[]{:S(2)}, u32[]{:S(2)}) %collective-permute-start.12) | collective-permute-done | bytes 147488 | tf_op jit(solution)/shard_map/ppermute | solution.py:693
  128.8 1.6 %collective-permute-done.11.g2 = f32[36,8,128]{2,1,0:T(8,128)S(1)} collective-permute-done((f32[36,8,128]{2,1,0:T(8,128)S(1)}, f32[36,8,128]{2,1,0:T(8,128)S(1)}, u32[]{:S(2)}, u32[]{:S(2)}) %collective-permute-start.11) | collective-permute-done | bytes 147488 | tf_op jit(solution)/shard_map/ppermute | solution.py:693
  130.5 2.0 %collective-permute-done.10.g1 = f32[36,8,128]{2,1,0:T(8,128)S(1)} collective-permute-done((f32[36,8,128]{2,1,0:T(8,128)S(1)}, f32[36,8,128]{2,1,0:T(8,128)S(1)}, u32[]{:S(2)}, u32[]{:S(2)}) %collective-permute-start.10) | collective-permute-done | bytes 147488 | tf_op jit(solution)/shard_map/ppermute | solution.py:693
  132.5 0.7 close.1
  (17 shorter events, 0.0 us)
Async XLA Ops:
  24.2 23.8 %collective-permute-start = (f32[2,129,8,128]{3,2,1,0:T(8,128)}, f32[2,129,8,128]{3,2,1,0:T(8,128)S(1)}, u32[]{:S(2)}, u32[]{:S(2)}) collective-permute-start(f32[2,129,8,128]{3,2,1,0:T(8,128)} %get-tuple-element.41), channel_id=1, source_target_pairs={{0,16},{1,65},{2,18},{3,67},{4,20},{5,69},{6,22},{7,71},{8,24},{9,... | collective-permute-start | bytes 3170312 | tf_op jit(solution)/shard_map/ppermute | solution.py:688
  26.5 25.6 %collective-permute-start.1 = (f32[2,129,8,128]{3,2,1,0:T(8,128)}, f32[2,129,8,128]{3,2,1,0:T(8,128)S(1)}, u32[]{:S(2)}, u32[]{:S(2)}) collective-permute-start(f32[2,129,8,128]{3,2,1,0:T(8,128)} %get-tuple-element.42), channel_id=1, source_target_pairs={{0,8},{1,33},{2,10},{3,35},{4,12},{5,37},{6,14},{7,39},{8,16},{9,4... | collective-permute-start | bytes 3170312 | tf_op jit(solution)/shard_map/ppermute | solution.py:688
  28.4 24.5 %collective-permute-start.2 = (f32[2,129,8,128]{3,2,1,0:T(8,128)}, f32[2,129,8,128]{3,2,1,0:T(8,128)}, u32[]{:S(2)}, u32[]{:S(2)}) collective-permute-start(f32[2,129,8,128]{3,2,1,0:T(8,128)} %get-tuple-element.43), channel_id=1, source_target_pairs={{0,24},{1,97},{2,26},{3,99},{4,28},{5,101},{6,30},{7,103},{8,0},{9... | collective-permute-start | bytes 3170312 | tf_op jit(solution)/shard_map/ppermute | solution.py:688
  29.8 23.2 %copy-start.1 = (f32[2,129,8,128]{3,2,1,0:T(8,128)S(1)}, f32[2,129,8,128]{3,2,1,0:T(8,128)}, u32[]{:S(2)}) copy-start(f32[2,129,8,128]{3,2,1,0:T(8,128)} %get-tuple-element.40.refs_0_) | copy-start | bytes 3170308
  46.2 19.7 %collective-permute-start.3 = (f32[2,129,8,128]{3,2,1,0:T(8,128)}, f32[2,129,8,128]{3,2,1,0:T(8,128)S(1)}, u32[]{:S(2)}, u32[]{:S(2)}) collective-permute-start(f32[2,129,8,128]{3,2,1,0:T(8,128)} %get-tuple-element.46), channel_id=1, source_target_pairs={{0,16},{1,65},{2,18},{3,67},{4,20},{5,69},{6,22},{7,71},{8,24},{9,... | collective-permute-start | bytes 3170312 | tf_op jit(solution)/shard_map/ppermute | solution.py:688
  47.8 38.3 %collective-permute-start.4 = (f32[2,129,8,128]{3,2,1,0:T(8,128)}, f32[2,129,8,128]{3,2,1,0:T(8,128)S(1)}, u32[]{:S(2)}, u32[]{:S(2)}) collective-permute-start(f32[2,129,8,128]{3,2,1,0:T(8,128)} %get-tuple-element.47), channel_id=1, source_target_pairs={{0,8},{1,33},{2,10},{3,35},{4,12},{5,37},{6,14},{7,39},{8,16},{9,4... | collective-permute-start | bytes 3170312 | tf_op jit(solution)/shard_map/ppermute | solution.py:688
  48.0 38.9 %collective-permute-start.5 = (f32[2,129,8,128]{3,2,1,0:T(8,128)}, f32[2,129,8,128]{3,2,1,0:T(8,128)S(1)}, u32[]{:S(2)}, u32[]{:S(2)}) collective-permute-start(f32[2,129,8,128]{3,2,1,0:T(8,128)} %get-tuple-element.48), channel_id=1, source_target_pairs={{0,24},{1,97},{2,26},{3,99},{4,28},{5,101},{6,30},{7,103},{8,0},{9... | collective-permute-start | bytes 3170312 | tf_op jit(solution)/shard_map/ppermute | solution.py:688
  51.1 35.8 %copy-start = (f32[2,129,8,128]{3,2,1,0:T(8,128)S(1)}, f32[2,129,8,128]{3,2,1,0:T(8,128)}, u32[]{:S(2)}) copy-start(f32[2,129,8,128]{3,2,1,0:T(8,128)} %get-tuple-element.45.refs_0_) | copy-start | bytes 3170308
  60.8 39.5 %collective-permute-start.6 = (f32[257,8,128]{2,1,0:T(8,128)}, f32[257,8,128]{2,1,0:T(8,128)S(1)}, u32[]{:S(2)}, u32[]{:S(2)}) collective-permute-start(f32[257,8,128]{2,1,0:T(8,128)} %get-tuple-element.44), channel_id=1, source_target_pairs={{0,32},{1,9},{2,34},{3,11},{4,36},{5,13},{6,38},{7,15},{8,40},{9,1... | collective-permute-start | bytes 3158024 | tf_op jit(solution)/shard_map/ppermute | solution.py:688
  60.9 34.3 %copy-start.10 = (s32[1,8,32]{2,1,0:T(8,128)S(1)}, s32[1,8,32]{2,1,0:T(8,128)}, u32[]{:S(2)}) copy-start(s32[1,8,32]{2,1,0:T(8,128)} %param.15) | copy-start | bytes 3076
  60.9 34.3 %copy-start.11 = (s32[1,8,32]{2,1,0:T(8,128)S(1)}, s32[1,8,32]{2,1,0:T(8,128)}, u32[]{:S(2)}) copy-start(s32[1,8,32]{2,1,0:T(8,128)} %param.14) | copy-start | bytes 3076
  60.9 34.4 %copy-start.12 = (f32[16,2]{0,1:T(2,128)S(1)}, f32[16,2]{0,1:T(2,128)}, u32[]{:S(2)}) copy-start(f32[16,2]{0,1:T(2,128)} %param.18) | copy-start | bytes 388
  60.9 34.4 %copy-start.7 = (f32[4,8,128]{2,1,0:T(8,128)S(1)}, f32[4,8,128]{2,1,0:T(8,128)}, u32[]{:S(2)}) copy-start(f32[4,8,128]{2,1,0:T(8,128)} %constant.71) | copy-start | bytes 49156
  60.9 34.4 %copy-start.8 = (f32[4,8,128]{2,1,0:T(8,128)S(1)}, f32[4,8,128]{2,1,0:T(8,128)}, u32[]{:S(2)}) copy-start(f32[4,8,128]{2,1,0:T(8,128)} %constant.69) | copy-start | bytes 49156
  60.9 34.4 %copy-start.9 = (f32[4,8,128]{2,1,0:T(8,128)S(1)}, f32[4,8,128]{2,1,0:T(8,128)}, u32[]{:S(2)}) copy-start(f32[4,8,128]{2,1,0:T(8,128)} %constant.67) | copy-start | bytes 49156
  60.9 35.5 %copy-start.4 = (s32[4]{0:T(128)S(1)}, s32[4]{0:T(128)}, u32[]{:S(2)}) copy-start(s32[4]{0:T(128)} %pad_add_fusion.refs_0_.here) | copy-start | bytes 52
  60.9 35.5 %copy-start.5 = (s32[1,256]{1,0:T(1,128)S(1)}, s32[1,256]{1,0:T(1,128)}, u32[]{:S(2)}) copy-start(s32[1,256]{1,0:T(1,128)} %param.16) | copy-start | bytes 3076
  61.0 35.5 %copy-start.6 = (s32[1,32]{1,0:T(1,128)S(1)}, s32[1,32]{1,0:T(1,128)}, u32[]{:S(2)}) copy-start(s32[1,32]{1,0:T(1,128)} %param.17) | copy-start | bytes 388
  61.0 39.3 %collective-permute-start.8 = (f32[257,8,128]{2,1,0:T(8,128)}, f32[257,8,128]{2,1,0:T(8,128)S(1)}, u32[]{:S(2)}, u32[]{:S(2)}) collective-permute-start(f32[257,8,128]{2,1,0:T(8,128)} %get-tuple-element.51), channel_id=1, source_target_pairs={{0,96},{1,25},{2,98},{3,27},{4,100},{5,29},{6,102},{7,31},{8,104},... | collective-permute-start | bytes 3158024 | tf_op jit(solution)/shard_map/ppermute | solution.py:688
  92.0 16.8 %copy-start.3 = (f32[2,8,8,128]{3,2,1,0:T(8,128)S(1)}, f32[2,8,8,128]{3,2,1,0:T(8,128)}, u32[]{:S(2)}) copy-start(f32[2,8,8,128]{3,2,1,0:T(8,128)} %constant.61.clone.rows) | copy-start | bytes 196612
  92.0 16.7 %collective-permute-start.7 = (f32[257,8,128]{2,1,0:T(8,128)}, f32[257,8,128]{2,1,0:T(8,128)}, u32[]{:S(2)}, u32[]{:S(2)}) collective-permute-start(f32[257,8,128]{2,1,0:T(8,128)} %get-tuple-element.50), channel_id=1, source_target_pairs={{0,64},{1,17},{2,66},{3,19},{4,68},{5,21},{6,70},{7,23},{8,72},{9,... | collective-permute-start | bytes 3158024 | tf_op jit(solution)/shard_map/ppermute | solution.py:688
  95.3 13.4 %copy-start.2 = (bf16[4,256,256]{2,1,0:T(8,128)(2,1)S(1)}, bf16[4,256,256]{2,1,0:T(8,128)(2,1)}, u32[]{:S(2)}) copy-start(bf16[4,256,256]{2,1,0:T(8,128)(2,1)} %constant.60.clone.both) | copy-start | bytes 1572868
  116.3 2.1 %collective-permute-start.9 = (f32[4,36,8,128]{3,2,1,0:T(8,128)S(1)}, f32[4,36,8,128]{3,2,1,0:T(8,128)S(1)}, u32[]{:S(2)}, u32[]{:S(2)}) collective-permute-start(f32[4,36,8,128]{3,2,1,0:T(8,128)S(1)} %get-tuple-element.58), channel_id=1, source_target_pairs={{0,1},{1,0},{2,3},{3,2},{4,5},{5,4},{6,7},{7,6},{8,9},{9,8},{10,11... | collective-permute-start | bytes 1769480 | tf_op jit(solution)/shard_map/ppermute | solution.py:787
  118.5 10.4 %collective-permute-start.12 = (f32[36,8,128]{2,1,0:T(8,128)S(1)}, f32[36,8,128]{2,1,0:T(8,128)S(1)}, u32[]{:S(2)}, u32[]{:S(2)}) collective-permute-start(f32[36,8,128]{2,1,0:T(8,128)S(1)} %get-tuple-element.63), channel_id=1, source_target_pairs={{0,6},{1,7},{2,0},{3,1},{4,2},{5,3},{6,4},{7,5},{8,14},{9,15},{10,... | collective-permute-start | bytes 442376 | tf_op jit(solution)/shard_map/ppermute | solution.py:693
  122.2 8.2 %collective-permute-start.11 = (f32[36,8,128]{2,1,0:T(8,128)S(1)}, f32[36,8,128]{2,1,0:T(8,128)S(1)}, u32[]{:S(2)}, u32[]{:S(2)}) collective-permute-start(f32[36,8,128]{2,1,0:T(8,128)S(1)} %get-tuple-element.64), channel_id=1, source_target_pairs={{0,4},{1,5},{2,6},{3,7},{4,0},{5,1},{6,2},{7,3},{8,12},{9,13},{10,... | collective-permute-start | bytes 442376 | tf_op jit(solution)/shard_map/ppermute | solution.py:693
  123.5 9.0 %collective-permute-start.10 = (f32[36,8,128]{2,1,0:T(8,128)S(1)}, f32[36,8,128]{2,1,0:T(8,128)S(1)}, u32[]{:S(2)}, u32[]{:S(2)}) collective-permute-start(f32[36,8,128]{2,1,0:T(8,128)S(1)} %get-tuple-element.65), channel_id=1, source_target_pairs={{0,2},{1,3},{2,4},{3,5},{4,6},{5,7},{6,0},{7,1},{8,10},{9,11},{10,... | collective-permute-start | bytes 442376 | tf_op jit(solution)/shard_map/ppermute | solution.py:693
where the time goes:
time: 135 us; the launch traced here: 133 us
  Pallas kernels  64.3 us (48%)
  waiting for transfers between devices  43.7 us (32%)
  starting transfers between devices  22.3 us (17%)
  other arithmetic  1.84 us (1%)
    pallas_call x2, Pallas kernels, expand(): pl.pallas_call(functools.partial(expand_kernel, chunk), out_shape=out_sha...  39.3 us
    ppermute x9, waiting for transfers between devices, hop(): return lax.ppermute(x, ('sfc', 'grp'), pairs)  32.9 us
    ppermute x9, starting transfers between devices, hop(): return lax.ppermute(x, ('sfc', 'grp'), pairs)  16.9 us
    pallas_call x2, Pallas kernels, gather(): pl.pallas_call(functools.partial(gather_kernel, wide), out_shape=[jax.Sha...  13 us
    ppermute x3, waiting for transfers between devices, around(): return lax.ppermute(x, 'grp', pairs)  8.76 us
    pallas_call x1, Pallas kernels, per_device(): pl.pallas_call(levels_kernel, out_shape=(tiles(leaf_count), tiles(4, SEAT...  7.6 us
    ppermute x3, starting transfers between devices, around(): return lax.ppermute(x, 'grp', pairs)  5.26 us
    pallas_call x1, Pallas kernels, per_device(): make_phases(here, slots, boxes, parent_cone[0], box_cone[0], jnp.cos(angl...  3.75 us
  transfers between devices with their start and end apart: 13, of which 10 were waited for; matrix products, arithmetic and copies ran while one was open for 1% of the time, Pallas kernels for 25%

commit v1 on v0

--- a/solution.py
+++ b/solution.py
@@ -92,7 +92,7 @@
     return lax.broadcasted_iota(i32, shape, len(shape) - 1)
 
 
-CHUNKS = ((1, 3), (2, 0))
+CHUNKS = ((2,), (1,), (3,), (0,))
 ORDER = tuple(m for chunk in CHUNKS for m in chunk)
 
 
@@ -468,6 +468,8 @@
     return total
 
 
+EARLY = 2
+
 SEATS = 36
 
 
@@ -718,17 +720,30 @@
     pts = pts.reshape(-1, 128)
     arrived = []
     routing = (here, bin_plan.reshape(bins // 128, 128), bin_leaf.reshape(bins // 128, 128))
+    held = [None] * 4
+    last = None
+
+    def collect(c, last):
+        got = [after(arrived[c][0], last)] + arrived[c][1:]
+        sums = gather(got, leaf_count)
+        for m, part in zip(CHUNKS[c], sums):
+            held[m] = hop(part, m, 1, groups) if m else part
+        return sums[0]
+
     for c in range(len(CHUNKS)):
         sent = expand(c, routing, pts, cap)
         if not c:
             *sent, table, labels = sent
             table = table.reshape(-1)
-        table = after(table, sent[0])
-        routing = (table, labels)
+        last = sent[0]
         moved = [sent[0]]
         for k in (2, 1, 3):
             moved.append(hop(sent[k], k, 0, groups))
         arrived.append(moved)
+        if c >= EARLY and c + 1 < len(CHUNKS):
+            last = collect(c - EARLY, last)
+        table = after(table, last)
+        routing = (table, labels)
 
     cone_angles = after(cone_angles, sent[0])
     directions = cone_vectors(cone_angles)
@@ -752,14 +767,8 @@
         here, slots, boxes, parent_cone[0], box_cone[0], jnp.cos(angle), jnp.sin(angle)
     )
 
-    held = [None] * 4
-    last = sent[0]
-    for c, chunk in enumerate(CHUNKS):
-        got = [after(arrived[c][0], last)] + arrived[c][1:]
-        sums = gather(got, leaf_count)
-        last = sums[0]
-        for m, part in zip(chunk, sums):
-            held[m] = hop(part, m, 1, groups) if m else part
+    for c in range(len(CHUNKS) - 1 - EARLY, len(CHUNKS)):
+        last = collect(c, last)
 
     leaves, mine, other = pl.pallas_call(
         levels_kernel,

time: 135 us -> 135 us (level)
  waiting for transfers between devices: 43.7 us -> 23.9 us
  Pallas kernels: 64.3 us -> 77.9 us
  starting transfers between devices: 22.3 us -> 25.7 us
  local copies, waits for them, and re-layouts: 0.23 us -> 2.94 us
    ppermute x9 -> x15, waiting for transfers between devices: 32.9 us -> 13.3 us  [hop(): return lax.ppermute(x, ('sfc', 'grp'), pairs)]
    pallas_call x2 -> x4, Pallas kernels: 39.3 us -> 48.1 us  [expand(): pl.pallas_call(functools.partial(expand_kernel, chunk), out_shape=out_sha...]
    pallas_call x2 -> x4, Pallas kernels: 13 us -> 18.3 us  [gather(): pl.pallas_call(functools.partial(gather_kernel, wide), out_shape=[jax.Sha...]
    ppermute x9 -> x15, starting transfers between devices: 16.9 us -> 20.9 us  [hop(): return lax.ppermute(x, ('sfc', 'grp'), pairs)]
    unnamed x26 -> x38, local copies, waits for them, and re-layouts: 0.07 us -> 2.79 us
  transfers between devices with their start and end apart: 13 -> 19, of which waited for: 10 -> 7; matrix products, arithmetic and copies ran while one was open for 1% -> 1% of each run, Pallas kernels for 25% -> 45%
where the time goes in v1:
time: 135 us; the launch traced here: 133 us
  Pallas kernels  77.9 us (58%)
  starting transfers between devices  25.7 us (19%)
  waiting for transfers between devices  23.9 us (18%)
  local copies, waits for them, and re-layouts  2.94 us (2%)
  other arithmetic  1.87 us (1%)
    pallas_call x4, Pallas kernels, expand(): pl.pallas_call(functools.partial(expand_kernel, chunk), out_shape=out_sha...  48.1 us
    ppermute x15, starting transfers between devices, hop(): return lax.ppermute(x, ('sfc', 'grp'), pairs)  20.9 us
    pallas_call x4, Pallas kernels, gather(): pl.pallas_call(functools.partial(gather_kernel, wide), out_shape=[jax.Sha...  18.3 us
    ppermute x15, waiting for transfers between devices, hop(): return lax.ppermute(x, ('sfc', 'grp'), pairs)  13.3 us
    ppermute x3, waiting for transfers between devices, around(): return lax.ppermute(x, 'grp', pairs)  8.59 us
    pallas_call x1, Pallas kernels, per_device(): pl.pallas_call(levels_kernel, out_shape=(tiles(leaf_count), tiles(4, SEAT...  7.02 us
    ppermute x3, starting transfers between devices, around(): return lax.ppermute(x, 'grp', pairs)  4.71 us
    pallas_call x1, Pallas kernels, per_device(): make_phases(here, slots, boxes, parent_cone[0], box_cone[0], jnp.cos(angl...  3.75 us
  transfers between devices with their start and end apart: 19, of which 7 were waited for; matrix products, arithmetic and copies ran while one was open for 1% of the time, Pallas kernels for 45%

profile of v1, /device:TPU:0, one launch (start us, length us, event | category | flops | bytes accessed | tf_op | source)
XLA Modules:
  0.0 133.4 jit_solution(1287492272007834421)
XLA Ops:
  0.7 0.7 pad_add_fusion.refs_0_.here
  1.3 10.6 %expand.4 = (f32[1,129,8,128]{3,2,1,0:T(8,128)}, f32[1,129,8,128]{3,2,1,0:T(8,128)}, f32[1,129,8,128]{3,2,1,0:T(8,128)}, f32[1,129,8,128]{3,2,1,0:T(8,128)}, s32[24,128]{1,0:T(8,128)}, /*index=5*/f32[16,8,128]{2,1,0:T(8,128)}) custom-call(s32[4]{0:T(128)} %pad_add_fusion.refs_0_.here, s32[8,128]{1,0:T(8,128)} %bitcast.52, s32[8,128]{1,0:T(8,128)} %bitcast.53, ...), custom_call_target="tpu_custom_call" | custom-call | flops 268435456 | bytes 8388608 | tf_op jit(solution)/shard_map/expand/pallas_call | solution.py:352
  11.9 2.8 %collective-permute-start = (f32[1,129,8,128]{3,2,1,0:T(8,128)}, f32[1,129,8,128]{3,2,1,0:T(8,128)S(1)}, u32[]{:S(2)}, u32[]{:S(2)}) collective-permute-start(f32[1,129,8,128]{3,2,1,0:T(8,128)} %get-tuple-element.49), channel_id=1, source_target_pairs={{0,16},{1,65},{2,18},{3,67},{4,20},{5,69},{6,22},{7,71},{8,24},{9,... | collective-permute-start | bytes 1585160 | tf_op jit(solution)/shard_map/ppermute | solution.py:690
  14.7 0.2 collective-permute-start.1
  14.9 3.1 %collective-permute-start.2 = (f32[1,129,8,128]{3,2,1,0:T(8,128)}, f32[1,129,8,128]{3,2,1,0:T(8,128)}, u32[]{:S(2)}, u32[]{:S(2)}) collective-permute-start(f32[1,129,8,128]{3,2,1,0:T(8,128)} %get-tuple-element.51), channel_id=1, source_target_pairs={{0,24},{1,97},{2,26},{3,99},{4,28},{5,101},{6,30},{7,103},{8,0},{9... | collective-permute-start | bytes 1585160 | tf_op jit(solution)/shard_map/ppermute | solution.py:690
  18.0 14.4 %expand.5 = (f32[1,129,8,128]{3,2,1,0:T(8,128)}, f32[1,129,8,128]{3,2,1,0:T(8,128)}, f32[1,129,8,128]{3,2,1,0:T(8,128)}, f32[1,129,8,128]{3,2,1,0:T(8,128)}) custom-call(s32[3072]{0:T(1024)} %bitcast.49, f32[16,8,128]{2,1,0:T(8,128)} %get-tuple-element.44.refs_1_, f32[10240,128]{1,0:T(8,128)} %bitcast.46), custom_call_target="tpu_custom_call" | custom-call | flops 268435456 | bytes 8388608 | tf_op jit(solution)/shard_map/expand/pallas_call | solution.py:352
  32.3 0.1 collective-permute-start.3
  32.4 1.6 %collective-permute-start.4 = (f32[1,129,8,128]{3,2,1,0:T(8,128)}, f32[1,129,8,128]{3,2,1,0:T(8,128)S(1)}, u32[]{:S(2)}, u32[]{:S(2)}) collective-permute-start(f32[1,129,8,128]{3,2,1,0:T(8,128)} %get-tuple-element.58), channel_id=1, source_target_pairs={{0,8},{1,33},{2,10},{3,35},{4,12},{5,37},{6,14},{7,39},{8,16},{9,4... | collective-permute-start | bytes 1585160 | tf_op jit(solution)/shard_map/ppermute | solution.py:690
  34.1 1.7 %collective-permute-start.5 = (f32[1,129,8,128]{3,2,1,0:T(8,128)}, f32[1,129,8,128]{3,2,1,0:T(8,128)}, u32[]{:S(2)}, u32[]{:S(2)}) collective-permute-start(f32[1,129,8,128]{3,2,1,0:T(8,128)} %get-tuple-element.59), channel_id=1, source_target_pairs={{0,24},{1,97},{2,26},{3,99},{4,28},{5,101},{6,30},{7,103},{8,0},{9... | collective-permute-start | bytes 1585160 | tf_op jit(solution)/shard_map/ppermute | solution.py:690
  35.7 11.9 %expand.6 = (f32[1,129,8,128]{3,2,1,0:T(8,128)}, f32[1,129,8,128]{3,2,1,0:T(8,128)}, f32[1,129,8,128]{3,2,1,0:T(8,128)}, f32[1,129,8,128]{3,2,1,0:T(8,128)}) custom-call(s32[3072]{0:T(1024)} %bitcast.50, f32[16,8,128]{2,1,0:T(8,128)} %get-tuple-element.44.refs_1_, f32[10240,128]{1,0:T(8,128)} %bitcast.47), custom_call_target="tpu_custom_call" | custom-call | flops 268435456 | bytes 8388608 | tf_op jit(solution)/shard_map/expand/pallas_call | solution.py:352
  47.7 0.9 copy-done.6
  48.5 1.8 %collective-permute-start.6 = (f32[1,129,8,128]{3,2,1,0:T(8,128)}, f32[1,129,8,128]{3,2,1,0:T(8,128)S(1)}, u32[]{:S(2)}, u32[]{:S(2)}) collective-permute-start(f32[1,129,8,128]{3,2,1,0:T(8,128)} %get-tuple-element.61), channel_id=1, source_target_pairs={{0,16},{1,65},{2,18},{3,67},{4,20},{5,69},{6,22},{7,71},{8,24},{9,... | collective-permute-start | bytes 1585160 | tf_op jit(solution)/shard_map/ppermute | solution.py:690
  50.4 3.2 %collective-permute-start.8 = (f32[1,129,8,128]{3,2,1,0:T(8,128)}, f32[1,129,8,128]{3,2,1,0:T(8,128)}, u32[]{:S(2)}, u32[]{:S(2)}) collective-permute-start(f32[1,129,8,128]{3,2,1,0:T(8,128)} %get-tuple-element.63), channel_id=1, source_target_pairs={{0,24},{1,97},{2,26},{3,99},{4,28},{5,101},{6,30},{7,103},{8,0},{9... | collective-permute-start | bytes 1585160 | tf_op jit(solution)/shard_map/ppermute | solution.py:690
  53.6 1.0 copy-done.7
  54.7 4.3 %gather.4 = f32[257,8,128]{2,1,0:T(8,128)} custom-call(f32[1,129,8,128]{3,2,1,0:T(8,128)S(1)} %copy-done.5, f32[1,129,8,128]{3,2,1,0:T(8,128)S(1)} %collective-permute-done.refs_1_, f32[1,129,8,128]{3,2,1,0:T(8,128)S(1)} %copy-done.7, f32[1,129,8,128]{3,2,1,0:T(8,128)} %collective-permute-done.2.refs_3_), custom_call_target="tpu_custom_call" | custom-call | flops 67108864 | bytes 4194304 | tf_op jit(solution)/shard_map/gather/pallas_call | solution.py:423
  59.0 11.2 %expand.7 = (f32[1,129,8,128]{3,2,1,0:T(8,128)}, f32[1,129,8,128]{3,2,1,0:T(8,128)}, f32[1,129,8,128]{3,2,1,0:T(8,128)}, f32[1,129,8,128]{3,2,1,0:T(8,128)}) custom-call(s32[3072]{0:T(1024)} %bitcast.51, f32[16,8,128]{2,1,0:T(8,128)} %get-tuple-element.44.refs_1_, f32[10240,128]{1,0:T(8,128)} %bitcast.48), custom_call_target="tpu_custom_call" | custom-call | flops 268435456 | bytes 8388608 | tf_op jit(solution)/shard_map/expand/pallas_call | solution.py:352
  70.3 4.2 %collective-permute-start.13 = (f32[257,8,128]{2,1,0:T(8,128)}, f32[257,8,128]{2,1,0:T(8,128)S(1)}, u32[]{:S(2)}, u32[]{:S(2)}) collective-permute-start(f32[257,8,128]{2,1,0:T(8,128)} %gather.4), channel_id=1, source_target_pairs={{0,64},{1,17},{2,66},{3,19},{4,68},{5,21},{6,70},{7,23},{8,72},{9,... | collective-permute-start | bytes 3158024 | tf_op jit(solution)/shard_map/ppermute | solution.py:690
  74.5 5.5 %gather.5 = f32[257,8,128]{2,1,0:T(8,128)} custom-call(f32[1,129,8,128]{3,2,1,0:T(8,128)S(1)} %copy-done.3, f32[1,129,8,128]{3,2,1,0:T(8,128)S(1)} %collective-permute-done.3.refs_1_, f32[1,129,8,128]{3,2,1,0:T(8,128)S(1)} %collective-permute-done.4.refs_2_, f32[1,129,8,128]{3,2,1,0:T(8,128)} %collective-permute-done.5.refs_3_), custom_call_target="tpu_custom_call" | custom-call | flops 67108864 | bytes 4194304 | tf_op jit(solution)/shard_map/gather/pallas_call | solution.py:423
  80.1 0.0 copy-start.13
  80.1 0.0 copy-start.14
  80.1 0.0 copy-start.15
  80.2 5.2 %gather.6 = f32[257,8,128]{2,1,0:T(8,128)} custom-call(f32[1,129,8,128]{3,2,1,0:T(8,128)S(1)} %copy-done.4, f32[1,129,8,128]{3,2,1,0:T(8,128)S(1)} %collective-permute-done.6.refs_1_, f32[1,129,8,128]{3,2,1,0:T(8,128)} %collective-permute-done.7.refs_2_, f32[1,129,8,128]{3,2,1,0:T(8,128)} %collective-permute-done.8.refs_3_), custom_call_target="tpu_custom_call" | custom-call | flops 67108864 | bytes 4194304 | tf_op jit(solution)/shard_map/gather/pallas_call | solution.py:423
  85.4 1.0 collective-permute-start.14
  86.4 1.1 collective-permute-start.12
  87.5 0.2 collective-permute-start.10
  87.6 3.5 %collective-permute-done.9.refs_1_ = f32[1,129,8,128]{3,2,1,0:T(8,128)S(1)} collective-permute-done((f32[1,129,8,128]{3,2,1,0:T(8,128)}, f32[1,129,8,128]{3,2,1,0:T(8,128)S(1)}, u32[]{:S(2)}, u32[]{:S(2)}) %collective-permute-start.9) | collective-permute-done | bytes 528416 | tf_op jit(solution)/shard_map/ppermute | solution.py:690
  91.2 0.8 copy-done.1
  92.0 0.1 reshape.81.boxes
  92.0 0.1 reshape.80.slots
  92.1 0.1 multiply_bitcast_fusion.1
  92.2 1.1 fusion
  93.3 3.8 %phases.1 = (f32[8,32,8,128]{3,2,1,0:T(8,128)S(1)}, f32[8,32,8,128]{3,2,1,0:T(8,128)S(1)}, f32[8,32,8,128]{3,2,1,0:T(8,128)S(1)}, f32[8,32,8,128]{3,2,1,0:T(8,12...) custom-call(s32[4]{0:T(128)S(1)} %copy-done.10, s32[256]{0:T(256)S(1)} %reshape.80.slots, ...), custom_call_target="tpu_custom_call" | custom-call | tf_op jit(solution)/shard_map/phases/pallas_call | solution.py:766
  97.1 0.0 copy-start.8
  97.1 0.0 copy-start.9
  97.1 7.1 %collective-permute-done.10.refs_2_ = f32[1,129,8,128]{3,2,1,0:T(8,128)} collective-permute-done((f32[1,129,8,128]{3,2,1,0:T(8,128)}, f32[1,129,8,128]{3,2,1,0:T(8,128)}, u32[]{:S(2)}, u32[]{:S(2)}) %collective-permute-start.10) | collective-permute-done | bytes 528416 | tf_op jit(solution)/shard_map/ppermute | solution.py:690
  104.2 2.7 %collective-permute-done.11.refs_3_ = f32[1,129,8,128]{3,2,1,0:T(8,128)} collective-permute-done((f32[1,129,8,128]{3,2,1,0:T(8,128)}, f32[1,129,8,128]{3,2,1,0:T(8,128)}, u32[]{:S(2)}, u32[]{:S(2)}) %collective-permute-start.11) | collective-permute-done | bytes 528416 | tf_op jit(solution)/shard_map/ppermute | solution.py:690
  106.9 3.2 %gather.7.a0 = f32[257,8,128]{2,1,0:T(8,128)S(1)} custom-call(f32[1,129,8,128]{3,2,1,0:T(8,128)S(1)} %copy-done, f32[1,129,8,128]{3,2,1,0:T(8,128)S(1)} %copy-done.2, f32[1,129,8,128]{3,2,1,0:T(8,128)} %collective-permute-done.10.refs_2_, f32[1,129,8,128]{3,2,1,0:T(8,128)} %collective-permute-done.11.refs_3_), custom_call_target="tpu_custom_call" | custom-call | flops 67108864 | bytes 4194304 | tf_op jit(solution)/shard_map/gather/pallas_call | solution.py:423
  110.2 7.0 %levels.1 = (f32[256,8,128]{2,1,0:T(8,128)}, f32[4,36,8,128]{3,2,1,0:T(8,128)S(1)}, f32[4,36,8,128]{3,2,1,0:T(8,128)S(1)}) custom-call(s32[4]{0:T(128)S(1)} %copy-done.10, s32[256]{0:T(256)S(1)} %get-tuple-element.55.goal, s32[256]{0:T(256)S(1)} %reshape.81.boxes, f32[257,8,128]{2,1,0:T(8,128)S(1)} %gather.7.a0, ...), custom_call_target="tpu_custom_call" | custom-call | tf_op jit(solution)/shard_map/levels/pallas_call | solution.py:773
  117.2 0.1 collective-permute-start.15
  117.3 2.0 %collective-permute-done.15 = f32[4,36,8,128]{3,2,1,0:T(8,128)S(1)} collective-permute-done((f32[4,36,8,128]{3,2,1,0:T(8,128)S(1)}, f32[4,36,8,128]{3,2,1,0:T(8,128)S(1)}, u32[]{:S(2)}, u32[]{:S(2)}) %collective-permute-start.15) | collective-permute-done | bytes 589856 | tf_op jit(solution)/shard_map/ppermute | solution.py:796
  119.3 0.1 fusion.2
  119.4 3.0 %collective-permute-start.18 = (f32[36,8,128]{2,1,0:T(8,128)S(1)}, f32[36,8,128]{2,1,0:T(8,128)S(1)}, u32[]{:S(2)}, u32[]{:S(2)}) collective-permute-start(f32[36,8,128]{2,1,0:T(8,128)S(1)} %get-tuple-element.79), channel_id=1, source_target_pairs={{0,6},{1,7},{2,0},{3,1},{4,2},{5,3},{6,4},{7,5},{8,14},{9,15},{10,... | collective-permute-start | bytes 442376 | tf_op jit(solution)/shard_map/ppermute | solution.py:695
  122.4 0.9 collective-permute-start.17
  123.3 0.8 collective-permute-start.16
  124.1 4.9 %collective-permute-done.18.g3 = f32[36,8,128]{2,1,0:T(8,128)S(1)} collective-permute-done((f32[36,8,128]{2,1,0:T(8,128)S(1)}, f32[36,8,128]{2,1,0:T(8,128)S(1)}, u32[]{:S(2)}, u32[]{:S(2)}) %collective-permute-start.18) | collective-permute-done | bytes 147488 | tf_op jit(solution)/shard_map/ppermute | solution.py:695
  129.0 1.7 %collective-permute-done.17.g2 = f32[36,8,128]{2,1,0:T(8,128)S(1)} collective-permute-done((f32[36,8,128]{2,1,0:T(8,128)S(1)}, f32[36,8,128]{2,1,0:T(8,128)S(1)}, u32[]{:S(2)}, u32[]{:S(2)}) %collective-permute-start.17) | collective-permute-done | bytes 147488 | tf_op jit(solution)/shard_map/ppermute | solution.py:695
  130.7 2.0 %collective-permute-done.16.g1 = f32[36,8,128]{2,1,0:T(8,128)S(1)} collective-permute-done((f32[36,8,128]{2,1,0:T(8,128)S(1)}, f32[36,8,128]{2,1,0:T(8,128)S(1)}, u32[]{:S(2)}, u32[]{:S(2)}) %collective-permute-start.16) | collective-permute-done | bytes 147488 | tf_op jit(solution)/shard_map/ppermute | solution.py:695
  132.7 0.7 close.1
  (45 shorter events, 0.1 us)
Async XLA Ops:
  11.9 22.1 %collective-permute-start = (f32[1,129,8,128]{3,2,1,0:T(8,128)}, f32[1,129,8,128]{3,2,1,0:T(8,128)S(1)}, u32[]{:S(2)}, u32[]{:S(2)}) collective-permute-start(f32[1,129,8,128]{3,2,1,0:T(8,128)} %get-tuple-element.49), channel_id=1, source_target_pairs={{0,16},{1,65},{2,18},{3,67},{4,20},{5,69},{6,22},{7,71},{8,24},{9,... | collective-permute-start | bytes 1585160 | tf_op jit(solution)/shard_map/ppermute | solution.py:690
  14.7 33.0 %collective-permute-start.1 = (f32[1,129,8,128]{3,2,1,0:T(8,128)}, f32[1,129,8,128]{3,2,1,0:T(8,128)S(1)}, u32[]{:S(2)}, u32[]{:S(2)}) collective-permute-start(f32[1,129,8,128]{3,2,1,0:T(8,128)} %get-tuple-element.50), channel_id=1, source_target_pairs={{0,8},{1,33},{2,10},{3,35},{4,12},{5,37},{6,14},{7,39},{8,16},{9,4... | collective-permute-start | bytes 1585160 | tf_op jit(solution)/shard_map/ppermute | solution.py:690
  14.9 35.5 %collective-permute-start.2 = (f32[1,129,8,128]{3,2,1,0:T(8,128)}, f32[1,129,8,128]{3,2,1,0:T(8,128)}, u32[]{:S(2)}, u32[]{:S(2)}) collective-permute-start(f32[1,129,8,128]{3,2,1,0:T(8,128)} %get-tuple-element.51), channel_id=1, source_target_pairs={{0,24},{1,97},{2,26},{3,99},{4,28},{5,101},{6,30},{7,103},{8,0},{9... | collective-permute-start | bytes 1585160 | tf_op jit(solution)/shard_map/ppermute | solution.py:690
  32.3 18.0 %collective-permute-start.3 = (f32[1,129,8,128]{3,2,1,0:T(8,128)}, f32[1,129,8,128]{3,2,1,0:T(8,128)S(1)}, u32[]{:S(2)}, u32[]{:S(2)}) collective-permute-start(f32[1,129,8,128]{3,2,1,0:T(8,128)} %get-tuple-element.57), channel_id=1, source_target_pairs={{0,16},{1,65},{2,18},{3,67},{4,20},{5,69},{6,22},{7,71},{8,24},{9,... | collective-permute-start | bytes 1585160 | tf_op jit(solution)/shard_map/ppermute | solution.py:690
  32.4 37.8 %collective-permute-start.4 = (f32[1,129,8,128]{3,2,1,0:T(8,128)}, f32[1,129,8,128]{3,2,1,0:T(8,128)S(1)}, u32[]{:S(2)}, u32[]{:S(2)}) collective-permute-start(f32[1,129,8,128]{3,2,1,0:T(8,128)} %get-tuple-element.58), channel_id=1, source_target_pairs={{0,8},{1,33},{2,10},{3,35},{4,12},{5,37},{6,14},{7,39},{8,16},{9,4... | collective-permute-start | bytes 1585160 | tf_op jit(solution)/shard_map/ppermute | solution.py:690
  34.1 19.6 %copy-start.5 = (f32[1,129,8,128]{3,2,1,0:T(8,128)S(1)}, f32[1,129,8,128]{3,2,1,0:T(8,128)}, u32[]{:S(2)}) copy-start(f32[1,129,8,128]{3,2,1,0:T(8,128)} %get-tuple-element.48.refs_0_) | copy-start | bytes 1585156
  34.1 40.4 %collective-permute-start.5 = (f32[1,129,8,128]{3,2,1,0:T(8,128)}, f32[1,129,8,128]{3,2,1,0:T(8,128)}, u32[]{:S(2)}, u32[]{:S(2)}) collective-permute-start(f32[1,129,8,128]{3,2,1,0:T(8,128)} %get-tuple-element.59), channel_id=1, source_target_pairs={{0,24},{1,97},{2,26},{3,99},{4,28},{5,101},{6,30},{7,103},{8,0},{9... | collective-permute-start | bytes 1585160 | tf_op jit(solution)/shard_map/ppermute | solution.py:690
  47.7 0.9 copy-start.6
  48.5 31.6 %collective-permute-start.6 = (f32[1,129,8,128]{3,2,1,0:T(8,128)}, f32[1,129,8,128]{3,2,1,0:T(8,128)S(1)}, u32[]{:S(2)}, u32[]{:S(2)}) collective-permute-start(f32[1,129,8,128]{3,2,1,0:T(8,128)} %get-tuple-element.61), channel_id=1, source_target_pairs={{0,16},{1,65},{2,18},{3,67},{4,20},{5,69},{6,22},{7,71},{8,24},{9,... | collective-permute-start | bytes 1585160 | tf_op jit(solution)/shard_map/ppermute | solution.py:690
  50.4 29.8 %collective-permute-start.7 = (f32[1,129,8,128]{3,2,1,0:T(8,128)}, f32[1,129,8,128]{3,2,1,0:T(8,128)}, u32[]{:S(2)}, u32[]{:S(2)}) collective-permute-start(f32[1,129,8,128]{3,2,1,0:T(8,128)} %get-tuple-element.62), channel_id=1, source_target_pairs={{0,8},{1,33},{2,10},{3,35},{4,12},{5,37},{6,14},{7,39},{8,16},{9,4... | collective-permute-start | bytes 1585160 | tf_op jit(solution)/shard_map/ppermute | solution.py:690
  50.4 29.8 %collective-permute-start.8 = (f32[1,129,8,128]{3,2,1,0:T(8,128)}, f32[1,129,8,128]{3,2,1,0:T(8,128)}, u32[]{:S(2)}, u32[]{:S(2)}) collective-permute-start(f32[1,129,8,128]{3,2,1,0:T(8,128)} %get-tuple-element.63), channel_id=1, source_target_pairs={{0,24},{1,97},{2,26},{3,99},{4,28},{5,101},{6,30},{7,103},{8,0},{9... | collective-permute-start | bytes 1585160 | tf_op jit(solution)/shard_map/ppermute | solution.py:690
  53.6 1.0 copy-start.7
  59.0 15.5 %copy-start.3 = (f32[1,129,8,128]{3,2,1,0:T(8,128)S(1)}, f32[1,129,8,128]{3,2,1,0:T(8,128)}, u32[]{:S(2)}) copy-start(f32[1,129,8,128]{3,2,1,0:T(8,128)} %get-tuple-element.56.refs_0_) | copy-start | bytes 1585156
  70.3 39.9 %collective-permute-start.13 = (f32[257,8,128]{2,1,0:T(8,128)}, f32[257,8,128]{2,1,0:T(8,128)S(1)}, u32[]{:S(2)}, u32[]{:S(2)}) collective-permute-start(f32[257,8,128]{2,1,0:T(8,128)} %gather.4), channel_id=1, source_target_pairs={{0,64},{1,17},{2,66},{3,19},{4,68},{5,21},{6,70},{7,23},{8,72},{9,... | collective-permute-start | bytes 3158024 | tf_op jit(solution)/shard_map/ppermute | solution.py:690
  74.5 5.7 %copy-start.4 = (f32[1,129,8,128]{3,2,1,0:T(8,128)S(1)}, f32[1,129,8,128]{3,2,1,0:T(8,128)}, u32[]{:S(2)}) copy-start(f32[1,129,8,128]{3,2,1,0:T(8,128)} %get-tuple-element.60.refs_0_) | copy-start | bytes 1585156
  74.5 16.7 %collective-permute-start.9 = (f32[1,129,8,128]{3,2,1,0:T(8,128)}, f32[1,129,8,128]{3,2,1,0:T(8,128)S(1)}, u32[]{:S(2)}, u32[]{:S(2)}) collective-permute-start(f32[1,129,8,128]{3,2,1,0:T(8,128)} %get-tuple-element.65), channel_id=1, source_target_pairs={{0,16},{1,65},{2,18},{3,67},{4,20},{5,69},{6,22},{7,71},{8,24},{9,... | collective-permute-start | bytes 1585160 | tf_op jit(solution)/shard_map/ppermute | solution.py:690
  80.0 12.0 %copy-start.16 = (s32[1,8,32]{2,1,0:T(8,128)S(1)}, s32[1,8,32]{2,1,0:T(8,128)}, u32[]{:S(2)}) copy-start(s32[1,8,32]{2,1,0:T(8,128)} %param.15) | copy-start | bytes 3076
  80.0 12.0 %copy-start.17 = (s32[1,8,32]{2,1,0:T(8,128)S(1)}, s32[1,8,32]{2,1,0:T(8,128)}, u32[]{:S(2)}) copy-start(s32[1,8,32]{2,1,0:T(8,128)} %param.14) | copy-start | bytes 3076
  80.0 12.1 %copy-start.18 = (f32[16,2]{0,1:T(2,128)S(1)}, f32[16,2]{0,1:T(2,128)}, u32[]{:S(2)}) copy-start(f32[16,2]{0,1:T(2,128)} %param.18) | copy-start | bytes 388
  80.1 12.1 %copy-start.13 = (f32[4,8,128]{2,1,0:T(8,128)S(1)}, f32[4,8,128]{2,1,0:T(8,128)}, u32[]{:S(2)}) copy-start(f32[4,8,128]{2,1,0:T(8,128)} %constant.71) | copy-start | bytes 49156
  80.1 12.1 %copy-start.14 = (f32[4,8,128]{2,1,0:T(8,128)S(1)}, f32[4,8,128]{2,1,0:T(8,128)}, u32[]{:S(2)}) copy-start(f32[4,8,128]{2,1,0:T(8,128)} %constant.69) | copy-start | bytes 49156
  80.1 12.1 %copy-start.15 = (f32[4,8,128]{2,1,0:T(8,128)S(1)}, f32[4,8,128]{2,1,0:T(8,128)}, u32[]{:S(2)}) copy-start(f32[4,8,128]{2,1,0:T(8,128)} %constant.67) | copy-start | bytes 49156
  80.1 13.2 %copy-start.10 = (s32[4]{0:T(128)S(1)}, s32[4]{0:T(128)}, u32[]{:S(2)}) copy-start(s32[4]{0:T(128)} %pad_add_fusion.refs_0_.here) | copy-start | bytes 52
  80.1 13.2 %copy-start.11 = (s32[1,256]{1,0:T(1,128)S(1)}, s32[1,256]{1,0:T(1,128)}, u32[]{:S(2)}) copy-start(s32[1,256]{1,0:T(1,128)} %param.16) | copy-start | bytes 3076
  80.1 13.2 %copy-start.12 = (s32[1,32]{1,0:T(1,128)S(1)}, s32[1,32]{1,0:T(1,128)}, u32[]{:S(2)}) copy-start(s32[1,32]{1,0:T(1,128)} %param.17) | copy-start | bytes 388
  85.4 24.8 %collective-permute-start.14 = (f32[257,8,128]{2,1,0:T(8,128)}, f32[257,8,128]{2,1,0:T(8,128)S(1)}, u32[]{:S(2)}, u32[]{:S(2)}) collective-permute-start(f32[257,8,128]{2,1,0:T(8,128)} %gather.6), channel_id=1, source_target_pairs={{0,96},{1,25},{2,98},{3,27},{4,100},{5,29},{6,102},{7,31},{8,104},... | collective-permute-start | bytes 3158024 | tf_op jit(solution)/shard_map/ppermute | solution.py:690
  86.4 23.8 %collective-permute-start.12 = (f32[257,8,128]{2,1,0:T(8,128)}, f32[257,8,128]{2,1,0:T(8,128)S(1)}, u32[]{:S(2)}, u32[]{:S(2)}) collective-permute-start(f32[257,8,128]{2,1,0:T(8,128)} %gather.5), channel_id=1, source_target_pairs={{0,32},{1,9},{2,34},{3,11},{4,36},{5,13},{6,38},{7,15},{8,40},{9,1... | collective-permute-start | bytes 3158024 | tf_op jit(solution)/shard_map/ppermute | solution.py:690
  87.5 16.7 %collective-permute-start.10 = (f32[1,129,8,128]{3,2,1,0:T(8,128)}, f32[1,129,8,128]{3,2,1,0:T(8,128)}, u32[]{:S(2)}, u32[]{:S(2)}) collective-permute-start(f32[1,129,8,128]{3,2,1,0:T(8,128)} %get-tuple-element.66), channel_id=1, source_target_pairs={{0,8},{1,33},{2,10},{3,35},{4,12},{5,37},{6,14},{7,39},{8,16},{9,4... | collective-permute-start | bytes 1585160 | tf_op jit(solution)/shard_map/ppermute | solution.py:690
  91.2 0.8 copy-start.1
  92.0 14.9 %collective-permute-start.11 = (f32[1,129,8,128]{3,2,1,0:T(8,128)}, f32[1,129,8,128]{3,2,1,0:T(8,128)}, u32[]{:S(2)}, u32[]{:S(2)}) collective-permute-start(f32[1,129,8,128]{3,2,1,0:T(8,128)} %get-tuple-element.67), channel_id=1, source_target_pairs={{0,24},{1,97},{2,26},{3,99},{4,28},{5,101},{6,30},{7,103},{8,0},{9... | collective-permute-start | bytes 1585160 | tf_op jit(solution)/shard_map/ppermute | solution.py:690
  92.1 14.8 %copy-start = (f32[1,129,8,128]{3,2,1,0:T(8,128)S(1)}, f32[1,129,8,128]{3,2,1,0:T(8,128)}, u32[]{:S(2)}) copy-start(f32[1,129,8,128]{3,2,1,0:T(8,128)} %get-tuple-element.64.refs_0_) | copy-start | bytes 1585156
  92.1 14.8 %copy-start.2 = (f32[1,129,8,128]{3,2,1,0:T(8,128)S(1)}, f32[1,129,8,128]{3,2,1,0:T(8,128)}, u32[]{:S(2)}) copy-start(f32[1,129,8,128]{3,2,1,0:T(8,128)} %copy-done.1) | copy-start | bytes 1585156
  97.1 13.1 %copy-start.8 = (bf16[4,256,256]{2,1,0:T(8,128)(2,1)S(1)}, bf16[4,256,256]{2,1,0:T(8,128)(2,1)}, u32[]{:S(2)}) copy-start(bf16[4,256,256]{2,1,0:T(8,128)(2,1)} %constant.60.clone.both) | copy-start | bytes 1572868
  97.1 13.1 %copy-start.9 = (f32[2,8,8,128]{3,2,1,0:T(8,128)S(1)}, f32[2,8,8,128]{3,2,1,0:T(8,128)}, u32[]{:S(2)}) copy-start(f32[2,8,8,128]{3,2,1,0:T(8,128)} %constant.61.clone.rows) | copy-start | bytes 196612
  117.2 2.1 %collective-permute-start.15 = (f32[4,36,8,128]{3,2,1,0:T(8,128)S(1)}, f32[4,36,8,128]{3,2,1,0:T(8,128)S(1)}, u32[]{:S(2)}, u32[]{:S(2)}) collective-permute-start(f32[4,36,8,128]{3,2,1,0:T(8,128)S(1)} %get-tuple-element.74), channel_id=1, source_target_pairs={{0,1},{1,0},{2,3},{3,2},{4,5},{5,4},{6,7},{7,6},{8,9},{9,8},{10,11... | collective-permute-start | bytes 1769480 | tf_op jit(solution)/shard_map/ppermute | solution.py:796
  119.4 9.6 %collective-permute-start.18 = (f32[36,8,128]{2,1,0:T(8,128)S(1)}, f32[36,8,128]{2,1,0:T(8,128)S(1)}, u32[]{:S(2)}, u32[]{:S(2)}) collective-permute-start(f32[36,8,128]{2,1,0:T(8,128)S(1)} %get-tuple-element.79), channel_id=1, source_target_pairs={{0,6},{1,7},{2,0},{3,1},{4,2},{5,3},{6,4},{7,5},{8,14},{9,15},{10,... | collective-permute-start | bytes 442376 | tf_op jit(solution)/shard_map/ppermute | solution.py:695
  122.4 8.3 %collective-permute-start.17 = (f32[36,8,128]{2,1,0:T(8,128)S(1)}, f32[36,8,128]{2,1,0:T(8,128)S(1)}, u32[]{:S(2)}, u32[]{:S(2)}) collective-permute-start(f32[36,8,128]{2,1,0:T(8,128)S(1)} %get-tuple-element.80), channel_id=1, source_target_pairs={{0,4},{1,5},{2,6},{3,7},{4,0},{5,1},{6,2},{7,3},{8,12},{9,13},{10,... | collective-permute-start | bytes 442376 | tf_op jit(solution)/shard_map/ppermute | solution.py:695
  123.3 9.4 %collective-permute-start.16 = (f32[36,8,128]{2,1,0:T(8,128)S(1)}, f32[36,8,128]{2,1,0:T(8,128)S(1)}, u32[]{:S(2)}, u32[]{:S(2)}) collective-permute-start(f32[36,8,128]{2,1,0:T(8,128)S(1)} %get-tuple-element.81), channel_id=1, source_target_pairs={{0,2},{1,3},{2,4},{3,5},{4,6},{5,7},{6,0},{7,1},{8,10},{9,11},{10,... | collective-permute-start | bytes 442376 | tf_op jit(solution)/shard_map/ppermute | solution.py:695

commit v2 on v1

--- a/solution.py
+++ b/solution.py
@@ -211,7 +211,11 @@
     outs, refs = refs[:4], refs[4:]
     if not chunk:
         listed, labels, *refs = refs
-    held, all_pts, stage, bx, by, bz, sems, load_sems, *refs = refs
+    held, stage, bx, by, bz, sems, *refs = refs
+    if chunk:
+        all_pts = pts
+    else:
+        all_pts, load_sems, *refs = refs
     first = sum(len(c) for c in CHUNKS[:chunk])
     wide = len(CHUNKS[chunk])
     rows = outs[0].shape[1]
@@ -222,7 +226,7 @@
             pts.at[pl.ds(span * axis, span)], all_pts.at[pl.ds(span * axis, span)],
             load_sems.at[axis],
         )
-        for axis in range(5)
+        for axis in range(0 if chunk else 5)
     ]
     for load in loads:
         load.start()
@@ -335,7 +339,7 @@
     out_specs = [ANY] * 4
     scratch = []
     if chunk:
-        in_specs = [SMEM, VMEM, ANY]
+        in_specs = [SMEM, VMEM, VMEM]
     else:
         in_specs = [SMEM, VMEM, VMEM, ANY]
         out_shape += [
@@ -344,6 +348,8 @@
         ]
         out_specs += [VMEM] * 2
         scratch = [
+            pltpu.VMEM(pts.shape, f32),
+            pltpu.SemaphoreType.DMA((5,)),
             pltpu.SMEM((24, 128), i32),
             pltpu.VMEM((128, 128), f32),
             pltpu.VMEM((128, 128), f32),
@@ -356,16 +362,15 @@
         out_specs=out_specs,
         scratch_shapes=[
             pltpu.VMEM((4 * wide * (cap + 1) + 1, 8, 128), f32),
-            pltpu.VMEM(pts.shape, f32),
             pltpu.VMEM((2, 3, 2, GROUP, 128), f32),
             *[pltpu.VMEM((2, 2, 8 * GROUP, 128), f32)] * 3,
             pltpu.SemaphoreType.DMA((4, wide)),
-            pltpu.SemaphoreType.DMA((5,)),
             *scratch,
         ],
         cost_estimate=pl.CostEstimate(
             flops=wide * (1 << 28), bytes_accessed=1 << 23, transcendentals=0
         ),
+        compiler_params=pltpu.CompilerParams(vmem_limit_bytes=(20 if chunk else 60) << 20),
         name="expand",
     )(*routing, pts)
 

time: 135 us -> 126 us (0.933)
  Pallas kernels: 77.9 us -> 64.9 us
  local copies, waits for them, and re-layouts: 2.94 us -> 5.08 us
  waiting for transfers between devices: 23.9 us -> 25.5 us
    pallas_call x4, Pallas kernels: 48.1 us -> 37.5 us  [expand(): pl.pallas_call(functools.partial(expand_kernel, chunk), out_shape=out_sha...]
    pallas_call x4, Pallas kernels: 18.3 us -> 15.9 us  [gather(): pl.pallas_call(functools.partial(gather_kernel, wide), out_shape=[jax.Sha...]
    unnamed x38 -> x42, local copies, waits for them, and re-layouts: 2.79 us -> 4.93 us
    ppermute x15, waiting for transfers between devices: 13.3 us -> 14.9 us  [hop(): return lax.ppermute(x, ('sfc', 'grp'), pairs)]
  transfers between devices with their start and end apart: 19 -> 19, of which waited for: 7 -> 7; matrix products, arithmetic and copies ran while one was open for 1% -> 1% of each run, Pallas kernels for 45% -> 38%
where the time goes in v2:
time: 126 us; the launch traced here: 124 us
  Pallas kernels  64.9 us (52%)
  starting transfers between devices  25.6 us (20%)
  waiting for transfers between devices  25.5 us (20%)
  local copies, waits for them, and re-layouts  5.08 us (4%)
  other arithmetic  1.82 us (1%)
    pallas_call x4, Pallas kernels, expand(): pl.pallas_call(functools.partial(expand_kernel, chunk), out_shape=out_sha...  37.5 us
    ppermute x15, starting transfers between devices, hop(): return lax.ppermute(x, ('sfc', 'grp'), pairs)  21.1 us
    pallas_call x4, Pallas kernels, gather(): pl.pallas_call(functools.partial(gather_kernel, wide), out_shape=[jax.Sha...  15.9 us
    ppermute x15, waiting for transfers between devices, hop(): return lax.ppermute(x, ('sfc', 'grp'), pairs)  14.9 us
    ppermute x3, waiting for transfers between devices, around(): return lax.ppermute(x, 'grp', pairs)  8.62 us
    pallas_call x1, Pallas kernels, per_device(): pl.pallas_call(levels_kernel, out_shape=(tiles(leaf_count), tiles(4, SEAT...  7.02 us
    unnamed x42, local copies, waits for them, and re-layouts  4.93 us
    ppermute x3, starting transfers between devices, around(): return lax.ppermute(x, 'grp', pairs)  4.51 us
  transfers between devices with their start and end apart: 19, of which 7 were waited for; matrix products, arithmetic and copies ran while one was open for 1% of the time, Pallas kernels for 38%

profile of v2, /device:TPU:0, one launch (start us, length us, event | category | flops | bytes accessed | tf_op | source)
XLA Modules:
  0.0 124.0 jit_solution(15005621949071890310)
XLA Ops:
  0.7 0.6 pad_add_fusion.refs_0_.here
  1.3 10.6 %expand.4 = (f32[1,129,8,128]{3,2,1,0:T(8,128)}, f32[1,129,8,128]{3,2,1,0:T(8,128)}, f32[1,129,8,128]{3,2,1,0:T(8,128)}, f32[1,129,8,128]{3,2,1,0:T(8,128)}, s32[24,128]{1,0:T(8,128)}, /*index=5*/f32[16,8,128]{2,1,0:T(8,128)}) custom-call(s32[4]{0:T(128)} %pad_add_fusion.refs_0_.here, s32[8,128]{1,0:T(8,128)} %bitcast.54, s32[8,128]{1,0:T(8,128)} %bitcast.55, ...), custom_call_target="tpu_custom_call" | custom-call | flops 268435456 | bytes 8388608 | tf_op jit(solution)/shard_map/expand/pallas_call | solution.py:358
  11.9 2.8 %collective-permute-start = (f32[1,129,8,128]{3,2,1,0:T(8,128)}, f32[1,129,8,128]{3,2,1,0:T(8,128)S(1)}, u32[]{:S(2)}, u32[]{:S(2)}) collective-permute-start(f32[1,129,8,128]{3,2,1,0:T(8,128)} %get-tuple-element.49), channel_id=1, source_target_pairs={{0,16},{1,65},{2,18},{3,67},{4,20},{5,69},{6,22},{7,71},{8,24},{9,... | collective-permute-start | bytes 1585160 | tf_op jit(solution)/shard_map/ppermute | solution.py:695
  14.7 0.2 collective-permute-start.1
  14.8 3.1 %collective-permute-start.2 = (f32[1,129,8,128]{3,2,1,0:T(8,128)}, f32[1,129,8,128]{3,2,1,0:T(8,128)S(1)}, u32[]{:S(2)}, u32[]{:S(2)}) collective-permute-start(f32[1,129,8,128]{3,2,1,0:T(8,128)} %get-tuple-element.51), channel_id=1, source_target_pairs={{0,24},{1,97},{2,26},{3,99},{4,28},{5,101},{6,30},{7,103},{8,0},{9... | collective-permute-start | bytes 1585160 | tf_op jit(solution)/shard_map/ppermute | solution.py:695
  17.9 2.5 %copy-done = f32[1024,5,256]{2,0,1:T(8,128)S(1)} copy-done((f32[1024,5,256]{2,0,1:T(8,128)S(1)}, f32[1024,5,256]{2,0,1:T(8,128)}, u32[]{:S(2)}) %copy-start) | copy-done | bytes 5242904
  20.4 0.8 copy-done.1
  21.2 0.7 copy-done.8
  21.9 10.6 %expand.5 = (f32[1,129,8,128]{3,2,1,0:T(8,128)S(1)}, f32[1,129,8,128]{3,2,1,0:T(8,128)S(1)}, f32[1,129,8,128]{3,2,1,0:T(8,128)S(1)}, f32[1,129,8,128]{3,2,1,0:T(8,128)S(1)}) custom-call(s32[3072]{0:T(1024)S(1)} %bitcast.49, f32[16,8,128]{2,1,0:T(8,128)S(1)} %copy-done.1, f32[10240,128]{1,0:T(8,128)S(1)} %bitcast.44), custom_call_target="tpu_custom_call" | custom-call | flops 268435456 | bytes 8388608 | tf_op jit(solution)/shard_map/expand/pallas_call | solution.py:358
  32.5 0.1 collective-permute-start.3
  32.6 1.6 %collective-permute-start.4 = (f32[1,129,8,128]{3,2,1,0:T(8,128)S(1)}, f32[1,129,8,128]{3,2,1,0:T(8,128)S(1)}, u32[]{:S(2)}, u32[]{:S(2)}) collective-permute-start(f32[1,129,8,128]{3,2,1,0:T(8,128)S(1)} %get-tuple-element.58), channel_id=1, source_target_pairs={{0,8},{1,33},{2,10},{3,35},{4,12},{5,37},{6,14},{7,39},{8,16},{9,4... | collective-permute-start | bytes 1585160 | tf_op jit(solution)/shard_map/ppermute | solution.py:695
  34.3 1.7 %collective-permute-start.5 = (f32[1,129,8,128]{3,2,1,0:T(8,128)S(1)}, f32[1,129,8,128]{3,2,1,0:T(8,128)S(1)}, u32[]{:S(2)}, u32[]{:S(2)}) collective-permute-start(f32[1,129,8,128]{3,2,1,0:T(8,128)S(1)} %get-tuple-element.59), channel_id=1, source_target_pairs={{0,24},{1,97},{2,26},{3,99},{4,28},{5,101},{6,30},{7,103},{8,0},{9... | collective-permute-start | bytes 1585160 | tf_op jit(solution)/shard_map/ppermute | solution.py:695
  36.0 8.1 %expand.6 = (f32[1,129,8,128]{3,2,1,0:T(8,128)S(1)}, f32[1,129,8,128]{3,2,1,0:T(8,128)S(1)}, f32[1,129,8,128]{3,2,1,0:T(8,128)S(1)}, f32[1,129,8,128]{3,2,1,0:T(8,128)S(1)}) custom-call(s32[3072]{0:T(1024)S(1)} %bitcast.50, f32[16,8,128]{2,1,0:T(8,128)S(1)} %copy-done.1, f32[10240,128]{1,0:T(8,128)S(1)} %bitcast.45), custom_call_target="tpu_custom_call" | custom-call | flops 268435456 | bytes 8388608 | tf_op jit(solution)/shard_map/expand/pallas_call | solution.py:358
  44.1 1.9 %collective-permute-start.6 = (f32[1,129,8,128]{3,2,1,0:T(8,128)S(1)}, f32[1,129,8,128]{3,2,1,0:T(8,128)S(1)}, u32[]{:S(2)}, u32[]{:S(2)}) collective-permute-start(f32[1,129,8,128]{3,2,1,0:T(8,128)S(1)} %get-tuple-element.61), channel_id=1, source_target_pairs={{0,16},{1,65},{2,18},{3,67},{4,20},{5,69},{6,22},{7,71},{8,24},{9,... | collective-permute-start | bytes 1585160 | tf_op jit(solution)/shard_map/ppermute | solution.py:695
  46.0 3.2 %collective-permute-start.8 = (f32[1,129,8,128]{3,2,1,0:T(8,128)S(1)}, f32[1,129,8,128]{3,2,1,0:T(8,128)S(1)}, u32[]{:S(2)}, u32[]{:S(2)}) collective-permute-start(f32[1,129,8,128]{3,2,1,0:T(8,128)S(1)} %get-tuple-element.63), channel_id=1, source_target_pairs={{0,24},{1,97},{2,26},{3,99},{4,28},{5,101},{6,30},{7,103},{8,0},{9... | collective-permute-start | bytes 1585160 | tf_op jit(solution)/shard_map/ppermute | solution.py:695
  49.2 3.6 %gather.4 = f32[257,8,128]{2,1,0:T(8,128)} custom-call(f32[1,129,8,128]{3,2,1,0:T(8,128)S(1)} %copy-done.6, f32[1,129,8,128]{3,2,1,0:T(8,128)S(1)} %collective-permute-done.refs_1_, f32[1,129,8,128]{3,2,1,0:T(8,128)S(1)} %collective-permute-done.1.refs_2_, f32[1,129,8,128]{3,2,1,0:T(8,128)S(1)} %collective-permute-done.2.refs_3_), custom_call_target="tpu_custom_call" | custom-call | flops 67108864 | bytes 4194304 | tf_op jit(solution)/shard_map/gather/pallas_call | solution.py:428
  52.9 8.2 %expand.7 = (f32[1,129,8,128]{3,2,1,0:T(8,128)S(1)}, f32[1,129,8,128]{3,2,1,0:T(8,128)}, f32[1,129,8,128]{3,2,1,0:T(8,128)S(1)}, f32[1,129,8,128]{3,2,1,0:T(8,128)}) custom-call(s32[3072]{0:T(1024)S(1)} %bitcast.51, f32[16,8,128]{2,1,0:T(8,128)S(1)} %copy-done.1, f32[10240,128]{1,0:T(8,128)S(1)} %bitcast.48), custom_call_target="tpu_custom_call" | custom-call | flops 268435456 | bytes 8388608 | tf_op jit(solution)/shard_map/expand/pallas_call | solution.py:358
  61.1 4.2 %collective-permute-start.13 = (f32[257,8,128]{2,1,0:T(8,128)}, f32[257,8,128]{2,1,0:T(8,128)S(1)}, u32[]{:S(2)}, u32[]{:S(2)}) collective-permute-start(f32[257,8,128]{2,1,0:T(8,128)} %gather.4), channel_id=1, source_target_pairs={{0,64},{1,17},{2,66},{3,19},{4,68},{5,21},{6,70},{7,23},{8,72},{9,... | collective-permute-start | bytes 3158024 | tf_op jit(solution)/shard_map/ppermute | solution.py:695
  65.3 4.8 %gather.5 = f32[257,8,128]{2,1,0:T(8,128)} custom-call(f32[1,129,8,128]{3,2,1,0:T(8,128)S(1)} %get-tuple-element.56.refs_0_, f32[1,129,8,128]{3,2,1,0:T(8,128)S(1)} %collective-permute-done.3.refs_1_, f32[1,129,8,128]{3,2,1,0:T(8,128)S(1)} %collective-permute-done.4.refs_2_, f32[1,129,8,128]{3,2,1,0:T(8,128)S(1)} %collective-permute-done.5.refs_3_), custom_call_target="tpu_custom_call" | custom-call | flops 67108864 | bytes 4194304 | tf_op jit(solution)/shard_map/gather/pallas_call | solution.py:428
  70.1 0.0 copy-start.13
  70.1 0.0 copy-start.15
  70.2 4.4 %gather.6 = f32[257,8,128]{2,1,0:T(8,128)} custom-call(f32[1,129,8,128]{3,2,1,0:T(8,128)S(1)} %get-tuple-element.60.refs_0_, f32[1,129,8,128]{3,2,1,0:T(8,128)S(1)} %collective-permute-done.6.refs_1_, f32[1,129,8,128]{3,2,1,0:T(8,128)S(1)} %collective-permute-done.7.refs_2_, f32[1,129,8,128]{3,2,1,0:T(8,128)S(1)} %collective-permute-done.8.refs_3_), custom_call_target="tpu_custom_call" | custom-call | flops 67108864 | bytes 4194304 | tf_op jit(solution)/shard_map/gather/pallas_call | solution.py:428
  74.5 1.0 collective-permute-start.14
  75.6 1.1 collective-permute-start.12
  76.6 0.2 collective-permute-start.10
  76.9 4.9 %collective-permute-done.9.refs_1_ = f32[1,129,8,128]{3,2,1,0:T(8,128)S(1)} collective-permute-done((f32[1,129,8,128]{3,2,1,0:T(8,128)S(1)}, f32[1,129,8,128]{3,2,1,0:T(8,128)S(1)}, u32[]{:S(2)}, u32[]{:S(2)}) %collective-permute-start.9) | collective-permute-done | bytes 528416 | tf_op jit(solution)/shard_map/ppermute | solution.py:695
  81.7 0.8 copy-done.4
  82.5 0.1 reshape.81.boxes
  82.6 0.1 reshape.80.slots
  82.7 0.1 multiply_bitcast_fusion.1
  82.8 1.1 fusion
  83.9 3.8 %phases.1 = (f32[8,32,8,128]{3,2,1,0:T(8,128)S(1)}, f32[8,32,8,128]{3,2,1,0:T(8,128)S(1)}, f32[8,32,8,128]{3,2,1,0:T(8,128)S(1)}, f32[8,32,8,128]{3,2,1,0:T(8,12...) custom-call(s32[4]{0:T(128)S(1)} %copy-done.10, s32[256]{0:T(256)S(1)} %reshape.80.slots, ...), custom_call_target="tpu_custom_call" | custom-call | tf_op jit(solution)/shard_map/phases/pallas_call | solution.py:771
  87.7 0.0 copy-start.7
  87.7 0.0 copy-start.9
  87.7 7.0 %collective-permute-done.10.refs_2_ = f32[1,129,8,128]{3,2,1,0:T(8,128)} collective-permute-done((f32[1,129,8,128]{3,2,1,0:T(8,128)}, f32[1,129,8,128]{3,2,1,0:T(8,128)}, u32[]{:S(2)}, u32[]{:S(2)}) %collective-permute-start.10) | collective-permute-done | bytes 528416 | tf_op jit(solution)/shard_map/ppermute | solution.py:695
  94.7 3.0 %collective-permute-done.11.refs_3_ = f32[1,129,8,128]{3,2,1,0:T(8,128)} collective-permute-done((f32[1,129,8,128]{3,2,1,0:T(8,128)}, f32[1,129,8,128]{3,2,1,0:T(8,128)}, u32[]{:S(2)}, u32[]{:S(2)}) %collective-permute-start.11) | collective-permute-done | bytes 528416 | tf_op jit(solution)/shard_map/ppermute | solution.py:695
  97.7 3.2 %gather.7.a0 = f32[257,8,128]{2,1,0:T(8,128)S(1)} custom-call(f32[1,129,8,128]{3,2,1,0:T(8,128)S(1)} %copy-done.3, f32[1,129,8,128]{3,2,1,0:T(8,128)S(1)} %copy-done.5, f32[1,129,8,128]{3,2,1,0:T(8,128)} %collective-permute-done.10.refs_2_, f32[1,129,8,128]{3,2,1,0:T(8,128)} %collective-permute-done.11.refs_3_), custom_call_target="tpu_custom_call" | custom-call | flops 67108864 | bytes 4194304 | tf_op jit(solution)/shard_map/gather/pallas_call | solution.py:428
  101.0 7.0 %levels.1 = (f32[256,8,128]{2,1,0:T(8,128)}, f32[4,36,8,128]{3,2,1,0:T(8,128)S(1)}, f32[4,36,8,128]{3,2,1,0:T(8,128)S(1)}) custom-call(s32[4]{0:T(128)S(1)} %copy-done.10, s32[256]{0:T(256)S(1)} %get-tuple-element.55.goal, s32[256]{0:T(256)S(1)} %reshape.81.boxes, f32[257,8,128]{2,1,0:T(8,128)S(1)} %gather.7.a0, ...), custom_call_target="tpu_custom_call" | custom-call | tf_op jit(solution)/shard_map/levels/pallas_call | solution.py:778
  108.0 0.1 collective-permute-start.15
  108.1 2.0 %collective-permute-done.15 = f32[4,36,8,128]{3,2,1,0:T(8,128)S(1)} collective-permute-done((f32[4,36,8,128]{3,2,1,0:T(8,128)S(1)}, f32[4,36,8,128]{3,2,1,0:T(8,128)S(1)}, u32[]{:S(2)}, u32[]{:S(2)}) %collective-permute-start.15) | collective-permute-done | bytes 589856 | tf_op jit(solution)/shard_map/ppermute | solution.py:801
  110.1 0.1 fusion.2
  110.2 2.9 %collective-permute-start.18 = (f32[36,8,128]{2,1,0:T(8,128)S(1)}, f32[36,8,128]{2,1,0:T(8,128)S(1)}, u32[]{:S(2)}, u32[]{:S(2)}) collective-permute-start(f32[36,8,128]{2,1,0:T(8,128)S(1)} %get-tuple-element.79), channel_id=1, source_target_pairs={{0,6},{1,7},{2,0},{3,1},{4,2},{5,3},{6,4},{7,5},{8,14},{9,15},{10,... | collective-permute-start | bytes 442376 | tf_op jit(solution)/shard_map/ppermute | solution.py:700
  113.0 0.8 collective-permute-start.17
  113.9 0.8 collective-permute-start.16
  114.7 4.9 %collective-permute-done.18.g3 = f32[36,8,128]{2,1,0:T(8,128)S(1)} collective-permute-done((f32[36,8,128]{2,1,0:T(8,128)S(1)}, f32[36,8,128]{2,1,0:T(8,128)S(1)}, u32[]{:S(2)}, u32[]{:S(2)}) %collective-permute-start.18) | collective-permute-done | bytes 147488 | tf_op jit(solution)/shard_map/ppermute | solution.py:700
  119.6 1.7 %collective-permute-done.17.g2 = f32[36,8,128]{2,1,0:T(8,128)S(1)} collective-permute-done((f32[36,8,128]{2,1,0:T(8,128)S(1)}, f32[36,8,128]{2,1,0:T(8,128)S(1)}, u32[]{:S(2)}, u32[]{:S(2)}) %collective-permute-start.17) | collective-permute-done | bytes 147488 | tf_op jit(solution)/shard_map/ppermute | solution.py:700
  121.3 2.0 %collective-permute-done.16.g1 = f32[36,8,128]{2,1,0:T(8,128)S(1)} collective-permute-done((f32[36,8,128]{2,1,0:T(8,128)S(1)}, f32[36,8,128]{2,1,0:T(8,128)S(1)}, u32[]{:S(2)}, u32[]{:S(2)}) %collective-permute-start.16) | collective-permute-done | bytes 147488 | tf_op jit(solution)/shard_map/ppermute | solution.py:700
  123.3 0.7 close.1
  (50 shorter events, 0.1 us)
Async XLA Ops:
  11.9 22.4 %collective-permute-start = (f32[1,129,8,128]{3,2,1,0:T(8,128)}, f32[1,129,8,128]{3,2,1,0:T(8,128)S(1)}, u32[]{:S(2)}, u32[]{:S(2)}) collective-permute-start(f32[1,129,8,128]{3,2,1,0:T(8,128)} %get-tuple-element.49), channel_id=1, source_target_pairs={{0,16},{1,65},{2,18},{3,67},{4,20},{5,69},{6,22},{7,71},{8,24},{9,... | collective-permute-start | bytes 1585160 | tf_op jit(solution)/shard_map/ppermute | solution.py:695
  14.7 29.4 %collective-permute-start.1 = (f32[1,129,8,128]{3,2,1,0:T(8,128)}, f32[1,129,8,128]{3,2,1,0:T(8,128)S(1)}, u32[]{:S(2)}, u32[]{:S(2)}) collective-permute-start(f32[1,129,8,128]{3,2,1,0:T(8,128)} %get-tuple-element.50), channel_id=1, source_target_pairs={{0,8},{1,33},{2,10},{3,35},{4,12},{5,37},{6,14},{7,39},{8,16},{9,4... | collective-permute-start | bytes 1585160 | tf_op jit(solution)/shard_map/ppermute | solution.py:695
  14.8 31.2 %collective-permute-start.2 = (f32[1,129,8,128]{3,2,1,0:T(8,128)}, f32[1,129,8,128]{3,2,1,0:T(8,128)S(1)}, u32[]{:S(2)}, u32[]{:S(2)}) collective-permute-start(f32[1,129,8,128]{3,2,1,0:T(8,128)} %get-tuple-element.51), channel_id=1, source_target_pairs={{0,24},{1,97},{2,26},{3,99},{4,28},{5,101},{6,30},{7,103},{8,0},{9... | collective-permute-start | bytes 1585160 | tf_op jit(solution)/shard_map/ppermute | solution.py:695
  17.9 2.5 %copy-start = (f32[1024,5,256]{2,0,1:T(8,128)S(1)}, f32[1024,5,256]{2,0,1:T(8,128)}, u32[]{:S(2)}) copy-start(f32[1024,5,256]{2,0,1:T(8,128)} %param.11) | copy-start | bytes 15728644
  20.4 0.8 copy-start.1
  21.2 0.7 copy-start.8
  21.9 30.9 %slice-start = ((s8[5242880]{0:T(1024)(128)(4,1)}), s8[4194304]{0:T(1024)(128)(4,1)S(1)}, s32[]{:S(2)}) async-start(s8[5242880]{0:T(1024)(128)(4,1)} %bitcast.46), calls=%async_computation | async-start | bytes 8388608
  32.5 13.5 %collective-permute-start.3 = (f32[1,129,8,128]{3,2,1,0:T(8,128)S(1)}, f32[1,129,8,128]{3,2,1,0:T(8,128)S(1)}, u32[]{:S(2)}, u32[]{:S(2)}) collective-permute-start(f32[1,129,8,128]{3,2,1,0:T(8,128)S(1)} %get-tuple-element.57), channel_id=1, source_target_pairs={{0,16},{1,65},{2,18},{3,67},{4,20},{5,69},{6,22},{7,71},{8,24},{9,... | collective-permute-start | bytes 1585160 | tf_op jit(solution)/shard_map/ppermute | solution.py:695
  32.6 28.4 %collective-permute-start.4 = (f32[1,129,8,128]{3,2,1,0:T(8,128)S(1)}, f32[1,129,8,128]{3,2,1,0:T(8,128)S(1)}, u32[]{:S(2)}, u32[]{:S(2)}) collective-permute-start(f32[1,129,8,128]{3,2,1,0:T(8,128)S(1)} %get-tuple-element.58), channel_id=1, source_target_pairs={{0,8},{1,33},{2,10},{3,35},{4,12},{5,37},{6,14},{7,39},{8,16},{9,4... | collective-permute-start | bytes 1585160 | tf_op jit(solution)/shard_map/ppermute | solution.py:695
  34.3 15.0 %copy-start.6 = (f32[1,129,8,128]{3,2,1,0:T(8,128)S(1)}, f32[1,129,8,128]{3,2,1,0:T(8,128)}, u32[]{:S(2)}) copy-start(f32[1,129,8,128]{3,2,1,0:T(8,128)} %get-tuple-element.48.refs_0_) | copy-start | bytes 1585156
  34.3 18.6 %slice-start.1 = ((s8[5242880]{0:T(1024)(128)(4,1)}), s8[1048576]{0:T(1024)(128)(4,1)S(1)}, s32[]{:S(2)}) async-start(s8[5242880]{0:T(1024)(128)(4,1)} %bitcast.46), calls=%async_computation.1 | async-start | bytes 2097152
  34.3 31.0 %collective-permute-start.5 = (f32[1,129,8,128]{3,2,1,0:T(8,128)S(1)}, f32[1,129,8,128]{3,2,1,0:T(8,128)S(1)}, u32[]{:S(2)}, u32[]{:S(2)}) collective-permute-start(f32[1,129,8,128]{3,2,1,0:T(8,128)S(1)} %get-tuple-element.59), channel_id=1, source_target_pairs={{0,24},{1,97},{2,26},{3,99},{4,28},{5,101},{6,30},{7,103},{8,0},{9... | collective-permute-start | bytes 1585160 | tf_op jit(solution)/shard_map/ppermute | solution.py:695
  44.1 26.0 %collective-permute-start.6 = (f32[1,129,8,128]{3,2,1,0:T(8,128)S(1)}, f32[1,129,8,128]{3,2,1,0:T(8,128)S(1)}, u32[]{:S(2)}, u32[]{:S(2)}) collective-permute-start(f32[1,129,8,128]{3,2,1,0:T(8,128)S(1)} %get-tuple-element.61), channel_id=1, source_target_pairs={{0,16},{1,65},{2,18},{3,67},{4,20},{5,69},{6,22},{7,71},{8,24},{9,... | collective-permute-start | bytes 1585160 | tf_op jit(solution)/shard_map/ppermute | solution.py:695
  46.0 24.1 %collective-permute-start.7 = (f32[1,129,8,128]{3,2,1,0:T(8,128)S(1)}, f32[1,129,8,128]{3,2,1,0:T(8,128)S(1)}, u32[]{:S(2)}, u32[]{:S(2)}) collective-permute-start(f32[1,129,8,128]{3,2,1,0:T(8,128)S(1)} %get-tuple-element.62), channel_id=1, source_target_pairs={{0,8},{1,33},{2,10},{3,35},{4,12},{5,37},{6,14},{7,39},{8,16},{9,4... | collective-permute-start | bytes 1585160 | tf_op jit(solution)/shard_map/ppermute | solution.py:695
  46.0 24.1 %collective-permute-start.8 = (f32[1,129,8,128]{3,2,1,0:T(8,128)S(1)}, f32[1,129,8,128]{3,2,1,0:T(8,128)S(1)}, u32[]{:S(2)}, u32[]{:S(2)}) collective-permute-start(f32[1,129,8,128]{3,2,1,0:T(8,128)S(1)} %get-tuple-element.63), channel_id=1, source_target_pairs={{0,24},{1,97},{2,26},{3,99},{4,28},{5,101},{6,30},{7,103},{8,0},{9... | collective-permute-start | bytes 1585160 | tf_op jit(solution)/shard_map/ppermute | solution.py:695
  61.0 9.0 %copy-start.2 = (f32[1,129,8,128]{3,2,1,0:T(8,128)}, f32[1,129,8,128]{3,2,1,0:T(8,128)S(1)}, u32[]{:S(2)}) copy-start(f32[1,129,8,128]{3,2,1,0:T(8,128)S(1)} %get-tuple-element.64.refs_0_) | copy-start | bytes 1585156
  61.1 39.9 %collective-permute-start.13 = (f32[257,8,128]{2,1,0:T(8,128)}, f32[257,8,128]{2,1,0:T(8,128)S(1)}, u32[]{:S(2)}, u32[]{:S(2)}) collective-permute-start(f32[257,8,128]{2,1,0:T(8,128)} %gather.4), channel_id=1, source_target_pairs={{0,64},{1,17},{2,66},{3,19},{4,68},{5,21},{6,70},{7,23},{8,72},{9,... | collective-permute-start | bytes 3158024 | tf_op jit(solution)/shard_map/ppermute | solution.py:695
  65.3 16.5 %collective-permute-start.9 = (f32[1,129,8,128]{3,2,1,0:T(8,128)S(1)}, f32[1,129,8,128]{3,2,1,0:T(8,128)S(1)}, u32[]{:S(2)}, u32[]{:S(2)}) collective-permute-start(f32[1,129,8,128]{3,2,1,0:T(8,128)S(1)} %get-tuple-element.65), channel_id=1, source_target_pairs={{0,16},{1,65},{2,18},{3,67},{4,20},{5,69},{6,22},{7,71},{8,24},{9,... | collective-permute-start | bytes 1585160 | tf_op jit(solution)/shard_map/ppermute | solution.py:695
  70.0 12.5 %copy-start.16 = (s32[1,8,32]{2,1,0:T(8,128)S(1)}, s32[1,8,32]{2,1,0:T(8,128)}, u32[]{:S(2)}) copy-start(s32[1,8,32]{2,1,0:T(8,128)} %param.15) | copy-start | bytes 3076
  70.0 12.6 %copy-start.17 = (s32[1,8,32]{2,1,0:T(8,128)S(1)}, s32[1,8,32]{2,1,0:T(8,128)}, u32[]{:S(2)}) copy-start(s32[1,8,32]{2,1,0:T(8,128)} %param.14) | copy-start | bytes 3076
  70.0 12.7 %copy-start.18 = (f32[16,2]{0,1:T(2,128)S(1)}, f32[16,2]{0,1:T(2,128)}, u32[]{:S(2)}) copy-start(f32[16,2]{0,1:T(2,128)} %param.18) | copy-start | bytes 388
  70.1 12.7 %copy-start.13 = (f32[4,8,128]{2,1,0:T(8,128)S(1)}, f32[4,8,128]{2,1,0:T(8,128)}, u32[]{:S(2)}) copy-start(f32[4,8,128]{2,1,0:T(8,128)} %constant.71) | copy-start | bytes 49156
  70.1 12.7 %copy-start.14 = (f32[4,8,128]{2,1,0:T(8,128)S(1)}, f32[4,8,128]{2,1,0:T(8,128)}, u32[]{:S(2)}) copy-start(f32[4,8,128]{2,1,0:T(8,128)} %constant.69) | copy-start | bytes 49156
  70.1 12.7 %copy-start.15 = (f32[4,8,128]{2,1,0:T(8,128)S(1)}, f32[4,8,128]{2,1,0:T(8,128)}, u32[]{:S(2)}) copy-start(f32[4,8,128]{2,1,0:T(8,128)} %constant.67) | copy-start | bytes 49156
  70.1 13.8 %copy-start.10 = (s32[4]{0:T(128)S(1)}, s32[4]{0:T(128)}, u32[]{:S(2)}) copy-start(s32[4]{0:T(128)} %pad_add_fusion.refs_0_.here) | copy-start | bytes 52
  70.1 13.8 %copy-start.11 = (s32[1,256]{1,0:T(1,128)S(1)}, s32[1,256]{1,0:T(1,128)}, u32[]{:S(2)}) copy-start(s32[1,256]{1,0:T(1,128)} %param.16) | copy-start | bytes 3076
  70.1 13.8 %copy-start.12 = (s32[1,32]{1,0:T(1,128)S(1)}, s32[1,32]{1,0:T(1,128)}, u32[]{:S(2)}) copy-start(s32[1,32]{1,0:T(1,128)} %param.17) | copy-start | bytes 388
  74.5 26.4 %collective-permute-start.14 = (f32[257,8,128]{2,1,0:T(8,128)}, f32[257,8,128]{2,1,0:T(8,128)S(1)}, u32[]{:S(2)}, u32[]{:S(2)}) collective-permute-start(f32[257,8,128]{2,1,0:T(8,128)} %gather.6), channel_id=1, source_target_pairs={{0,96},{1,25},{2,98},{3,27},{4,100},{5,29},{6,102},{7,31},{8,104},... | collective-permute-start | bytes 3158024 | tf_op jit(solution)/shard_map/ppermute | solution.py:695
  75.6 25.3 %collective-permute-start.12 = (f32[257,8,128]{2,1,0:T(8,128)}, f32[257,8,128]{2,1,0:T(8,128)S(1)}, u32[]{:S(2)}, u32[]{:S(2)}) collective-permute-start(f32[257,8,128]{2,1,0:T(8,128)} %gather.5), channel_id=1, source_target_pairs={{0,32},{1,9},{2,34},{3,11},{4,36},{5,13},{6,38},{7,15},{8,40},{9,1... | collective-permute-start | bytes 3158024 | tf_op jit(solution)/shard_map/ppermute | solution.py:695
  76.6 18.1 %collective-permute-start.10 = (f32[1,129,8,128]{3,2,1,0:T(8,128)}, f32[1,129,8,128]{3,2,1,0:T(8,128)}, u32[]{:S(2)}, u32[]{:S(2)}) collective-permute-start(f32[1,129,8,128]{3,2,1,0:T(8,128)} %get-tuple-element.66), channel_id=1, source_target_pairs={{0,8},{1,33},{2,10},{3,35},{4,12},{5,37},{6,14},{7,39},{8,16},{9,4... | collective-permute-start | bytes 1585160 | tf_op jit(solution)/shard_map/ppermute | solution.py:695
  81.7 0.8 copy-start.4
  82.5 15.2 %collective-permute-start.11 = (f32[1,129,8,128]{3,2,1,0:T(8,128)}, f32[1,129,8,128]{3,2,1,0:T(8,128)}, u32[]{:S(2)}, u32[]{:S(2)}) collective-permute-start(f32[1,129,8,128]{3,2,1,0:T(8,128)} %get-tuple-element.67), channel_id=1, source_target_pairs={{0,24},{1,97},{2,26},{3,99},{4,28},{5,101},{6,30},{7,103},{8,0},{9... | collective-permute-start | bytes 1585160 | tf_op jit(solution)/shard_map/ppermute | solution.py:695
  82.7 15.0 %copy-start.3 = (f32[1,129,8,128]{3,2,1,0:T(8,128)S(1)}, f32[1,129,8,128]{3,2,1,0:T(8,128)}, u32[]{:S(2)}) copy-start(f32[1,129,8,128]{3,2,1,0:T(8,128)} %copy-done.2) | copy-start | bytes 1585156
  82.7 15.0 %copy-start.5 = (f32[1,129,8,128]{3,2,1,0:T(8,128)S(1)}, f32[1,129,8,128]{3,2,1,0:T(8,128)}, u32[]{:S(2)}) copy-start(f32[1,129,8,128]{3,2,1,0:T(8,128)} %copy-done.4) | copy-start | bytes 1585156
  87.7 13.3 %copy-start.7 = (bf16[4,256,256]{2,1,0:T(8,128)(2,1)S(1)}, bf16[4,256,256]{2,1,0:T(8,128)(2,1)}, u32[]{:S(2)}) copy-start(bf16[4,256,256]{2,1,0:T(8,128)(2,1)} %constant.60.clone.both) | copy-start | bytes 1572868
  87.7 13.3 %copy-start.9 = (f32[2,8,8,128]{3,2,1,0:T(8,128)S(1)}, f32[2,8,8,128]{3,2,1,0:T(8,128)}, u32[]{:S(2)}) copy-start(f32[2,8,8,128]{3,2,1,0:T(8,128)} %constant.61.clone.rows) | copy-start | bytes 196612
  108.0 2.1 %collective-permute-start.15 = (f32[4,36,8,128]{3,2,1,0:T(8,128)S(1)}, f32[4,36,8,128]{3,2,1,0:T(8,128)S(1)}, u32[]{:S(2)}, u32[]{:S(2)}) collective-permute-start(f32[4,36,8,128]{3,2,1,0:T(8,128)S(1)} %get-tuple-element.74), channel_id=1, source_target_pairs={{0,1},{1,0},{2,3},{3,2},{4,5},{5,4},{6,7},{7,6},{8,9},{9,8},{10,11... | collective-permute-start | bytes 1769480 | tf_op jit(solution)/shard_map/ppermute | solution.py:801
  110.2 9.5 %collective-permute-start.18 = (f32[36,8,128]{2,1,0:T(8,128)S(1)}, f32[36,8,128]{2,1,0:T(8,128)S(1)}, u32[]{:S(2)}, u32[]{:S(2)}) collective-permute-start(f32[36,8,128]{2,1,0:T(8,128)S(1)} %get-tuple-element.79), channel_id=1, source_target_pairs={{0,6},{1,7},{2,0},{3,1},{4,2},{5,3},{6,4},{7,5},{8,14},{9,15},{10,... | collective-permute-start | bytes 442376 | tf_op jit(solution)/shard_map/ppermute | solution.py:700
  113.0 8.3 %collective-permute-start.17 = (f32[36,8,128]{2,1,0:T(8,128)S(1)}, f32[36,8,128]{2,1,0:T(8,128)S(1)}, u32[]{:S(2)}, u32[]{:S(2)}) collective-permute-start(f32[36,8,128]{2,1,0:T(8,128)S(1)} %get-tuple-element.80), channel_id=1, source_target_pairs={{0,4},{1,5},{2,6},{3,7},{4,0},{5,1},{6,2},{7,3},{8,12},{9,13},{10,... | collective-permute-start | bytes 442376 | tf_op jit(solution)/shard_map/ppermute | solution.py:700
  113.9 9.5 %collective-permute-start.16 = (f32[36,8,128]{2,1,0:T(8,128)S(1)}, f32[36,8,128]{2,1,0:T(8,128)S(1)}, u32[]{:S(2)}, u32[]{:S(2)}) collective-permute-start(f32[36,8,128]{2,1,0:T(8,128)S(1)} %get-tuple-element.81), channel_id=1, source_target_pairs={{0,2},{1,3},{2,4},{3,5},{4,6},{5,7},{6,0},{7,1},{8,10},{9,11},{10,... | collective-permute-start | bytes 442376 | tf_op jit(solution)/shard_map/ppermute | solution.py:700

commit v3 on v2

--- a/solution.py
+++ b/solution.py
@@ -341,7 +341,7 @@
     if chunk:
         in_specs = [SMEM, VMEM, VMEM]
     else:
-        in_specs = [SMEM, VMEM, VMEM, ANY]
+        in_specs = [SMEM, VMEM, VMEM, pl.BlockSpec(memory_space=pltpu.HBM)]
         out_shape += [
             jax.ShapeDtypeStruct((24, 128), i32),
             jax.ShapeDtypeStruct((16, 8, 128), f32),
@@ -370,7 +370,7 @@
         cost_estimate=pl.CostEstimate(
             flops=wide * (1 << 28), bytes_accessed=1 << 23, transcendentals=0
         ),
-        compiler_params=pltpu.CompilerParams(vmem_limit_bytes=(20 if chunk else 60) << 20),
+        compiler_params=pltpu.CompilerParams(vmem_limit_bytes=20 << 20),
         name="expand",
     )(*routing, pts)
 
@@ -473,7 +473,7 @@
     return total
 
 
-EARLY = 2
+EARLY = 3
 
 SEATS = 36
 

time: 126 us -> 128 us (1.016)
  starting transfers between devices: 25.6 us -> 29.9 us
  Pallas kernels: 64.9 us -> 62.7 us
  waiting for transfers between devices: 25.5 us -> 27.2 us
    ppermute x15, starting transfers between devices: 21.1 us -> 23.9 us  [hop(): return lax.ppermute(x, ('sfc', 'grp'), pairs)]
    pallas_call x4, Pallas kernels: 37.5 us -> 35.3 us  [expand(): pl.pallas_call(functools.partial(expand_kernel, chunk), out_shape=out_sha...]
    ppermute x15, waiting for transfers between devices: 14.9 us -> 17 us  [hop(): return lax.ppermute(x, ('sfc', 'grp'), pairs)]
    ppermute x3, starting transfers between devices: 4.51 us -> 5.98 us  [around(): return lax.ppermute(x, 'grp', pairs)]
    unnamed x42 -> x36, local copies, waits for them, and re-layouts: 4.93 us -> 4.75 us
  transfers between devices with their start and end apart: 19 -> 19, of which waited for: 7 -> 5; matrix products, arithmetic and copies ran while one was open for 1% -> 1% of each run, Pallas kernels for 38% -> 37%
where the time goes in v3:
time: 128 us; the launch traced here: 127 us
  Pallas kernels  62.7 us (49%)
  starting transfers between devices  29.9 us (23%)
  waiting for transfers between devices  27.2 us (21%)
  local copies, waits for them, and re-layouts  4.9 us (4%)
  other arithmetic  1.3 us (1%)
    pallas_call x4, Pallas kernels, expand(): pl.pallas_call(functools.partial(expand_kernel, chunk), out_shape=out_sha...  35.3 us
    ppermute x15, starting transfers between devices, hop(): return lax.ppermute(x, ('sfc', 'grp'), pairs)  23.9 us
    ppermute x15, waiting for transfers between devices, hop(): return lax.ppermute(x, ('sfc', 'grp'), pairs)  17 us
    pallas_call x4, Pallas kernels, gather(): pl.pallas_call(functools.partial(gather_kernel, wide), out_shape=[jax.Sha...  16 us
    ppermute x3, waiting for transfers between devices, around(): return lax.ppermute(x, 'grp', pairs)  8.25 us
    pallas_call x1, Pallas kernels, per_device(): pl.pallas_call(levels_kernel, out_shape=(tiles(leaf_count), tiles(4, SEAT...  7.02 us
    ppermute x3, starting transfers between devices, around(): return lax.ppermute(x, 'grp', pairs)  5.98 us
    unnamed x36, local copies, waits for them, and re-layouts  4.75 us
  transfers between devices with their start and end apart: 19, of which 5 were waited for; matrix products, arithmetic and copies ran while one was open for 1% of the time, Pallas kernels for 37%

profile of v3, /device:TPU:0, one launch (start us, length us, event | category | flops | bytes accessed | tf_op | source)
XLA Modules:
  0.0 127.1 jit_solution(11919895888513992946)
XLA Ops:
  0.7 0.1 pad_add_fusion.refs_0_.here
  0.7 2.5 %copy-done = f32[1024,5,256]{2,0,1:T(8,128)S(1)} copy-done((f32[1024,5,256]{2,0,1:T(8,128)S(1)}, f32[1024,5,256]{2,0,1:T(8,128)}, u32[]{:S(2)}) %copy-start) | copy-done | bytes 5242904
  3.2 0.7 copy-done.8
  3.9 0.7 copy-done.9
  4.6 8.4 %expand.4 = (f32[1,129,8,128]{3,2,1,0:T(8,128)S(1)}, f32[1,129,8,128]{3,2,1,0:T(8,128)S(1)}, f32[1,129,8,128]{3,2,1,0:T(8,128)S(1)}, f32[1,129,8,128]{3,2,1,0:T(...) custom-call(s32[4]{0:T(128)S(1)} %pad_add_fusion.refs_0_.here, s32[8,128]{1,0:T(8,128)S(1)} %bitcast.50, ...), custom_call_target="tpu_custom_call" | custom-call | flops 268435456 | bytes 8388608 | tf_op jit(solution)/shard_map/expand/pallas_call | solution.py:358
  13.0 2.8 %collective-permute-start = (f32[1,129,8,128]{3,2,1,0:T(8,128)S(1)}, f32[1,129,8,128]{3,2,1,0:T(8,128)S(1)}, u32[]{:S(2)}, u32[]{:S(2)}) collective-permute-start(f32[1,129,8,128]{3,2,1,0:T(8,128)S(1)} %get-tuple-element.53), channel_id=1, source_target_pairs={{0,16},{1,65},{2,18},{3,67},{4,20},{5,69},{6,22},{7,71},{8,24},{9,... | collective-permute-start | bytes 1585160 | tf_op jit(solution)/shard_map/ppermute | solution.py:695
  15.8 0.2 collective-permute-start.1
  16.0 3.1 %collective-permute-start.2 = (f32[1,129,8,128]{3,2,1,0:T(8,128)S(1)}, f32[1,129,8,128]{3,2,1,0:T(8,128)S(1)}, u32[]{:S(2)}, u32[]{:S(2)}) collective-permute-start(f32[1,129,8,128]{3,2,1,0:T(8,128)S(1)} %get-tuple-element.55), channel_id=1, source_target_pairs={{0,24},{1,97},{2,26},{3,99},{4,28},{5,101},{6,30},{7,103},{8,0},{9... | collective-permute-start | bytes 1585160 | tf_op jit(solution)/shard_map/ppermute | solution.py:695
  19.1 10.6 %expand.5 = (f32[1,129,8,128]{3,2,1,0:T(8,128)S(1)}, f32[1,129,8,128]{3,2,1,0:T(8,128)S(1)}, f32[1,129,8,128]{3,2,1,0:T(8,128)S(1)}, f32[1,129,8,128]{3,2,1,0:T(8,128)S(1)}) custom-call(s32[3072]{0:T(1024)S(1)} %bitcast.47, f32[16,8,128]{2,1,0:T(8,128)S(1)} %get-tuple-element.44.refs_1_, f32[10240,128]{1,0:T(8,128)S(1)} %bitcast.44), custom_call_target="tpu_custom_call" | custom-call | flops 268435456 | bytes 8388608 | tf_op jit(solution)/shard_map/expand/pallas_call | solution.py:358
  29.7 0.1 collective-permute-start.3
  29.8 1.6 %collective-permute-start.4 = (f32[1,129,8,128]{3,2,1,0:T(8,128)S(1)}, f32[1,129,8,128]{3,2,1,0:T(8,128)S(1)}, u32[]{:S(2)}, u32[]{:S(2)}) collective-permute-start(f32[1,129,8,128]{3,2,1,0:T(8,128)S(1)} %get-tuple-element.58), channel_id=1, source_target_pairs={{0,8},{1,33},{2,10},{3,35},{4,12},{5,37},{6,14},{7,39},{8,16},{9,4... | collective-permute-start | bytes 1585160 | tf_op jit(solution)/shard_map/ppermute | solution.py:695
  31.4 1.7 %collective-permute-start.5 = (f32[1,129,8,128]{3,2,1,0:T(8,128)S(1)}, f32[1,129,8,128]{3,2,1,0:T(8,128)S(1)}, u32[]{:S(2)}, u32[]{:S(2)}) collective-permute-start(f32[1,129,8,128]{3,2,1,0:T(8,128)S(1)} %get-tuple-element.59), channel_id=1, source_target_pairs={{0,24},{1,97},{2,26},{3,99},{4,28},{5,101},{6,30},{7,103},{8,0},{9... | collective-permute-start | bytes 1585160 | tf_op jit(solution)/shard_map/ppermute | solution.py:695
  33.1 8.1 %expand.6 = (f32[1,129,8,128]{3,2,1,0:T(8,128)S(1)}, f32[1,129,8,128]{3,2,1,0:T(8,128)S(1)}, f32[1,129,8,128]{3,2,1,0:T(8,128)S(1)}, f32[1,129,8,128]{3,2,1,0:T(8,128)S(1)}) custom-call(s32[3072]{0:T(1024)S(1)} %bitcast.48, f32[16,8,128]{2,1,0:T(8,128)S(1)} %get-tuple-element.44.refs_1_, f32[10240,128]{1,0:T(8,128)S(1)} %bitcast.45), custom_call_target="tpu_custom_call" | custom-call | flops 268435456 | bytes 8388608 | tf_op jit(solution)/shard_map/expand/pallas_call | solution.py:358
  41.2 1.9 %collective-permute-start.6 = (f32[1,129,8,128]{3,2,1,0:T(8,128)S(1)}, f32[1,129,8,128]{3,2,1,0:T(8,128)S(1)}, u32[]{:S(2)}, u32[]{:S(2)}) collective-permute-start(f32[1,129,8,128]{3,2,1,0:T(8,128)S(1)} %get-tuple-element.61), channel_id=1, source_target_pairs={{0,16},{1,65},{2,18},{3,67},{4,20},{5,69},{6,22},{7,71},{8,24},{9,... | collective-permute-start | bytes 1585160 | tf_op jit(solution)/shard_map/ppermute | solution.py:695
  43.1 3.2 %collective-permute-start.8 = (f32[1,129,8,128]{3,2,1,0:T(8,128)S(1)}, f32[1,129,8,128]{3,2,1,0:T(8,128)S(1)}, u32[]{:S(2)}, u32[]{:S(2)}) collective-permute-start(f32[1,129,8,128]{3,2,1,0:T(8,128)S(1)} %get-tuple-element.63), channel_id=1, source_target_pairs={{0,24},{1,97},{2,26},{3,99},{4,28},{5,101},{6,30},{7,103},{8,0},{9... | collective-permute-start | bytes 1585160 | tf_op jit(solution)/shard_map/ppermute | solution.py:695
  46.4 8.1 %expand.7 = (f32[1,129,8,128]{3,2,1,0:T(8,128)S(1)}, f32[1,129,8,128]{3,2,1,0:T(8,128)}, f32[1,129,8,128]{3,2,1,0:T(8,128)S(1)}, f32[1,129,8,128]{3,2,1,0:T(8,128)}) custom-call(s32[3072]{0:T(1024)S(1)} %bitcast.49, f32[16,8,128]{2,1,0:T(8,128)S(1)} %get-tuple-element.44.refs_1_, f32[10240,128]{1,0:T(8,128)S(1)} %bitcast.46), custom_call_target="tpu_custom_call" | custom-call | flops 268435456 | bytes 8388608 | tf_op jit(solution)/shard_map/expand/pallas_call | solution.py:358
  54.5 3.6 %gather.4 = f32[257,8,128]{2,1,0:T(8,128)} custom-call(f32[1,129,8,128]{3,2,1,0:T(8,128)S(1)} %get-tuple-element.52.refs_0_, f32[1,129,8,128]{3,2,1,0:T(8,128)S(1)} %collective-permute-done.refs_1_, f32[1,129,8,128]{3,2,1,0:T(8,128)S(1)} %collective-permute-done.1.refs_2_, f32[1,129,8,128]{3,2,1,0:T(8,128)S(1)} %collective-permute-done.2.refs_3_), custom_call_target="tpu_custom_call" | custom-call | flops 67108864 | bytes 4194304 | tf_op jit(solution)/shard_map/gather/pallas_call | solution.py:428
  58.2 1.3 %collective-permute-start.9 = (f32[1,129,8,128]{3,2,1,0:T(8,128)S(1)}, f32[1,129,8,128]{3,2,1,0:T(8,128)S(1)}, u32[]{:S(2)}, u32[]{:S(2)}) collective-permute-start(f32[1,129,8,128]{3,2,1,0:T(8,128)S(1)} %get-tuple-element.65), channel_id=1, source_target_pairs={{0,16},{1,65},{2,18},{3,67},{4,20},{5,69},{6,22},{7,71},{8,24},{9,... | collective-permute-start | bytes 1585160 | tf_op jit(solution)/shard_map/ppermute | solution.py:695
  59.5 4.8 %gather.5 = f32[257,8,128]{2,1,0:T(8,128)} custom-call(f32[1,129,8,128]{3,2,1,0:T(8,128)S(1)} %get-tuple-element.56.refs_0_, f32[1,129,8,128]{3,2,1,0:T(8,128)S(1)} %collective-permute-done.3.refs_1_, f32[1,129,8,128]{3,2,1,0:T(8,128)S(1)} %collective-permute-done.4.refs_2_, f32[1,129,8,128]{3,2,1,0:T(8,128)S(1)} %collective-permute-done.5.refs_3_), custom_call_target="tpu_custom_call" | custom-call | flops 67108864 | bytes 4194304 | tf_op jit(solution)/shard_map/gather/pallas_call | solution.py:428
  64.3 0.0 copy-start.12
  64.3 0.0 copy-start.13
  64.3 0.0 copy-start.14
  64.4 4.4 %gather.6 = f32[257,8,128]{2,1,0:T(8,128)} custom-call(f32[1,129,8,128]{3,2,1,0:T(8,128)S(1)} %get-tuple-element.60.refs_0_, f32[1,129,8,128]{3,2,1,0:T(8,128)S(1)} %collective-permute-done.6.refs_1_, f32[1,129,8,128]{3,2,1,0:T(8,128)S(1)} %collective-permute-done.7.refs_2_, f32[1,129,8,128]{3,2,1,0:T(8,128)S(1)} %collective-permute-done.8.refs_3_), custom_call_target="tpu_custom_call" | custom-call | flops 67108864 | bytes 4194304 | tf_op jit(solution)/shard_map/gather/pallas_call | solution.py:428
  68.8 0.8 collective-permute-start.14
  69.5 1.3 %collective-permute-start.12 = (f32[257,8,128]{2,1,0:T(8,128)}, f32[257,8,128]{2,1,0:T(8,128)S(1)}, u32[]{:S(2)}, u32[]{:S(2)}) collective-permute-start(f32[257,8,128]{2,1,0:T(8,128)} %gather.5), channel_id=1, source_target_pairs={{0,32},{1,9},{2,34},{3,11},{4,36},{5,13},{6,38},{7,15},{8,40},{9,1... | collective-permute-start | bytes 3158024 | tf_op jit(solution)/shard_map/ppermute | solution.py:695
  70.9 2.6 %collective-permute-start.13 = (f32[257,8,128]{2,1,0:T(8,128)}, f32[257,8,128]{2,1,0:T(8,128)S(1)}, u32[]{:S(2)}, u32[]{:S(2)}) collective-permute-start(f32[257,8,128]{2,1,0:T(8,128)} %gather.4), channel_id=1, source_target_pairs={{0,64},{1,17},{2,66},{3,19},{4,68},{5,21},{6,70},{7,23},{8,72},{9,... | collective-permute-start | bytes 3158024 | tf_op jit(solution)/shard_map/ppermute | solution.py:695
  73.5 0.8 copy-done.4
  74.3 3.2 %collective-permute-start.11 = (f32[1,129,8,128]{3,2,1,0:T(8,128)}, f32[1,129,8,128]{3,2,1,0:T(8,128)}, u32[]{:S(2)}, u32[]{:S(2)}) collective-permute-start(f32[1,129,8,128]{3,2,1,0:T(8,128)} %get-tuple-element.67), channel_id=1, source_target_pairs={{0,24},{1,97},{2,26},{3,99},{4,28},{5,101},{6,30},{7,103},{8,0},{9... | collective-permute-start | bytes 1585160 | tf_op jit(solution)/shard_map/ppermute | solution.py:695
  77.6 0.1 reshape.81.boxes
  77.7 0.1 reshape.80.slots
  77.7 0.1 multiply_bitcast_fusion.1
  77.8 1.1 fusion
  78.9 3.8 %phases.1 = (f32[8,32,8,128]{3,2,1,0:T(8,128)S(1)}, f32[8,32,8,128]{3,2,1,0:T(8,128)S(1)}, f32[8,32,8,128]{3,2,1,0:T(8,128)S(1)}, f32[8,32,8,128]{3,2,1,0:T(8,12...) custom-call(s32[4]{0:T(128)S(1)} %pad_add_fusion.refs_0_.here, ...), custom_call_target="tpu_custom_call" | custom-call | tf_op jit(solution)/shard_map/phases/pallas_call | solution.py:771
  82.7 0.0 copy-start.6
  82.7 0.0 copy-start.7
  82.7 16.9 %collective-permute-done.10.refs_2_ = f32[1,129,8,128]{3,2,1,0:T(8,128)} collective-permute-done((f32[1,129,8,128]{3,2,1,0:T(8,128)}, f32[1,129,8,128]{3,2,1,0:T(8,128)}, u32[]{:S(2)}, u32[]{:S(2)}) %collective-permute-start.10) | collective-permute-done | bytes 528416 | tf_op jit(solution)/shard_map/ppermute | solution.py:695
  99.6 3.2 %gather.7.a0 = f32[257,8,128]{2,1,0:T(8,128)S(1)} custom-call(f32[1,129,8,128]{3,2,1,0:T(8,128)S(1)} %copy-done.3, f32[1,129,8,128]{3,2,1,0:T(8,128)S(1)} %copy-done.5, f32[1,129,8,128]{3,2,1,0:T(8,128)} %collective-permute-done.10.refs_2_, f32[1,129,8,128]{3,2,1,0:T(8,128)} %collective-permute-done.11.refs_3_), custom_call_target="tpu_custom_call" | custom-call | flops 67108864 | bytes 4194304 | tf_op jit(solution)/shard_map/gather/pallas_call | solution.py:428
  102.9 7.0 %levels.1 = (f32[256,8,128]{2,1,0:T(8,128)}, f32[4,36,8,128]{3,2,1,0:T(8,128)S(1)}, f32[4,36,8,128]{3,2,1,0:T(8,128)S(1)}) custom-call(s32[4]{0:T(128)S(1)} %pad_add_fusion.refs_0_.here, s32[256]{0:T(256)S(1)} %get-tuple-element.51.goal, s32[256]{0:T(256)S(1)} %reshape.81.boxes, f32[257,8,128]{2,1,0:T(8,128)S(1)} %gather.7.a0, ...), custom_call_target="tpu_custom_call" | custom-call | tf_op jit(solution)/shard_map/levels/pallas_call | solution.py:778
  109.9 0.1 collective-permute-start.15
  110.0 2.0 %collective-permute-done.15 = f32[4,36,8,128]{3,2,1,0:T(8,128)S(1)} collective-permute-done((f32[4,36,8,128]{3,2,1,0:T(8,128)S(1)}, f32[4,36,8,128]{3,2,1,0:T(8,128)S(1)}, u32[]{:S(2)}, u32[]{:S(2)}) %collective-permute-start.15) | collective-permute-done | bytes 589856 | tf_op jit(solution)/shard_map/ppermute | solution.py:801
  112.0 0.1 fusion.2
  112.1 4.0 %collective-permute-start.18 = (f32[36,8,128]{2,1,0:T(8,128)S(1)}, f32[36,8,128]{2,1,0:T(8,128)S(1)}, u32[]{:S(2)}, u32[]{:S(2)}) collective-permute-start(f32[36,8,128]{2,1,0:T(8,128)S(1)} %get-tuple-element.79), channel_id=1, source_target_pairs={{0,6},{1,7},{2,0},{3,1},{4,2},{5,3},{6,4},{7,5},{8,14},{9,15},{10,... | collective-permute-start | bytes 442376 | tf_op jit(solution)/shard_map/ppermute | solution.py:700
  116.1 1.1 collective-permute-start.17
  117.2 0.9 collective-permute-start.16
  118.1 4.6 %collective-permute-done.18.g3 = f32[36,8,128]{2,1,0:T(8,128)S(1)} collective-permute-done((f32[36,8,128]{2,1,0:T(8,128)S(1)}, f32[36,8,128]{2,1,0:T(8,128)S(1)}, u32[]{:S(2)}, u32[]{:S(2)}) %collective-permute-start.18) | collective-permute-done | bytes 147488 | tf_op jit(solution)/shard_map/ppermute | solution.py:700
  122.7 1.6 %collective-permute-done.17.g2 = f32[36,8,128]{2,1,0:T(8,128)S(1)} collective-permute-done((f32[36,8,128]{2,1,0:T(8,128)S(1)}, f32[36,8,128]{2,1,0:T(8,128)S(1)}, u32[]{:S(2)}, u32[]{:S(2)}) %collective-permute-start.17) | collective-permute-done | bytes 147488 | tf_op jit(solution)/shard_map/ppermute | solution.py:700
  124.3 2.0 %collective-permute-done.16.g1 = f32[36,8,128]{2,1,0:T(8,128)S(1)} collective-permute-done((f32[36,8,128]{2,1,0:T(8,128)S(1)}, f32[36,8,128]{2,1,0:T(8,128)S(1)}, u32[]{:S(2)}, u32[]{:S(2)}) %collective-permute-start.16) | collective-permute-done | bytes 147488 | tf_op jit(solution)/shard_map/ppermute | solution.py:700
  126.4 0.7 close.1
  (43 shorter events, 0.1 us)
Async XLA Ops:
  0.7 2.5 %copy-start = (f32[1024,5,256]{2,0,1:T(8,128)S(1)}, f32[1024,5,256]{2,0,1:T(8,128)}, u32[]{:S(2)}) copy-start(f32[1024,5,256]{2,0,1:T(8,128)} %param.11) | copy-start | bytes 15728644
  3.2 0.7 copy-start.8
  3.9 0.7 copy-start.9
  4.6 14.5 %copy-start.1 = (f32[1024,5,256]{2,0,1:T(8,128)S(1)}, f32[1024,5,256]{2,0,1:T(8,128)}, u32[]{:S(2)}) copy-start(f32[1024,5,256]{2,0,1:T(8,128)} %param.11) | copy-start | bytes 15728644
  13.0 18.3 %collective-permute-start = (f32[1,129,8,128]{3,2,1,0:T(8,128)S(1)}, f32[1,129,8,128]{3,2,1,0:T(8,128)S(1)}, u32[]{:S(2)}, u32[]{:S(2)}) collective-permute-start(f32[1,129,8,128]{3,2,1,0:T(8,128)S(1)} %get-tuple-element.53), channel_id=1, source_target_pairs={{0,16},{1,65},{2,18},{3,67},{4,20},{5,69},{6,22},{7,71},{8,24},{9,... | collective-permute-start | bytes 1585160 | tf_op jit(solution)/shard_map/ppermute | solution.py:695
  15.8 25.4 %collective-permute-start.1 = (f32[1,129,8,128]{3,2,1,0:T(8,128)S(1)}, f32[1,129,8,128]{3,2,1,0:T(8,128)S(1)}, u32[]{:S(2)}, u32[]{:S(2)}) collective-permute-start(f32[1,129,8,128]{3,2,1,0:T(8,128)S(1)} %get-tuple-element.54), channel_id=1, source_target_pairs={{0,8},{1,33},{2,10},{3,35},{4,12},{5,37},{6,14},{7,39},{8,16},{9,4... | collective-permute-start | bytes 1585160 | tf_op jit(solution)/shard_map/ppermute | solution.py:695
  16.0 27.1 %collective-permute-start.2 = (f32[1,129,8,128]{3,2,1,0:T(8,128)S(1)}, f32[1,129,8,128]{3,2,1,0:T(8,128)S(1)}, u32[]{:S(2)}, u32[]{:S(2)}) collective-permute-start(f32[1,129,8,128]{3,2,1,0:T(8,128)S(1)} %get-tuple-element.55), channel_id=1, source_target_pairs={{0,24},{1,97},{2,26},{3,99},{4,28},{5,101},{6,30},{7,103},{8,0},{9... | collective-permute-start | bytes 1585160 | tf_op jit(solution)/shard_map/ppermute | solution.py:695
  29.7 13.4 %collective-permute-start.3 = (f32[1,129,8,128]{3,2,1,0:T(8,128)S(1)}, f32[1,129,8,128]{3,2,1,0:T(8,128)S(1)}, u32[]{:S(2)}, u32[]{:S(2)}) collective-permute-start(f32[1,129,8,128]{3,2,1,0:T(8,128)S(1)} %get-tuple-element.57), channel_id=1, source_target_pairs={{0,16},{1,65},{2,18},{3,67},{4,20},{5,69},{6,22},{7,71},{8,24},{9,... | collective-permute-start | bytes 1585160 | tf_op jit(solution)/shard_map/ppermute | solution.py:695
  29.8 28.4 %collective-permute-start.4 = (f32[1,129,8,128]{3,2,1,0:T(8,128)S(1)}, f32[1,129,8,128]{3,2,1,0:T(8,128)S(1)}, u32[]{:S(2)}, u32[]{:S(2)}) collective-permute-start(f32[1,129,8,128]{3,2,1,0:T(8,128)S(1)} %get-tuple-element.58), channel_id=1, source_target_pairs={{0,8},{1,33},{2,10},{3,35},{4,12},{5,37},{6,14},{7,39},{8,16},{9,4... | collective-permute-start | bytes 1585160 | tf_op jit(solution)/shard_map/ppermute | solution.py:695
  31.4 28.1 %collective-permute-start.5 = (f32[1,129,8,128]{3,2,1,0:T(8,128)S(1)}, f32[1,129,8,128]{3,2,1,0:T(8,128)S(1)}, u32[]{:S(2)}, u32[]{:S(2)}) collective-permute-start(f32[1,129,8,128]{3,2,1,0:T(8,128)S(1)} %get-tuple-element.59), channel_id=1, source_target_pairs={{0,24},{1,97},{2,26},{3,99},{4,28},{5,101},{6,30},{7,103},{8,0},{9... | collective-permute-start | bytes 1585160 | tf_op jit(solution)/shard_map/ppermute | solution.py:695
  41.2 23.1 %collective-permute-start.6 = (f32[1,129,8,128]{3,2,1,0:T(8,128)S(1)}, f32[1,129,8,128]{3,2,1,0:T(8,128)S(1)}, u32[]{:S(2)}, u32[]{:S(2)}) collective-permute-start(f32[1,129,8,128]{3,2,1,0:T(8,128)S(1)} %get-tuple-element.61), channel_id=1, source_target_pairs={{0,16},{1,65},{2,18},{3,67},{4,20},{5,69},{6,22},{7,71},{8,24},{9,... | collective-permute-start | bytes 1585160 | tf_op jit(solution)/shard_map/ppermute | solution.py:695
  43.1 21.2 %collective-permute-start.7 = (f32[1,129,8,128]{3,2,1,0:T(8,128)S(1)}, f32[1,129,8,128]{3,2,1,0:T(8,128)S(1)}, u32[]{:S(2)}, u32[]{:S(2)}) collective-permute-start(f32[1,129,8,128]{3,2,1,0:T(8,128)S(1)} %get-tuple-element.62), channel_id=1, source_target_pairs={{0,8},{1,33},{2,10},{3,35},{4,12},{5,37},{6,14},{7,39},{8,16},{9,4... | collective-permute-start | bytes 1585160 | tf_op jit(solution)/shard_map/ppermute | solution.py:695
  43.1 21.2 %collective-permute-start.8 = (f32[1,129,8,128]{3,2,1,0:T(8,128)S(1)}, f32[1,129,8,128]{3,2,1,0:T(8,128)S(1)}, u32[]{:S(2)}, u32[]{:S(2)}) collective-permute-start(f32[1,129,8,128]{3,2,1,0:T(8,128)S(1)} %get-tuple-element.63), channel_id=1, source_target_pairs={{0,24},{1,97},{2,26},{3,99},{4,28},{5,101},{6,30},{7,103},{8,0},{9... | collective-permute-start | bytes 1585160 | tf_op jit(solution)/shard_map/ppermute | solution.py:695
  54.5 3.6 %copy-start.2 = (f32[1,129,8,128]{3,2,1,0:T(8,128)}, f32[1,129,8,128]{3,2,1,0:T(8,128)S(1)}, u32[]{:S(2)}) copy-start(f32[1,129,8,128]{3,2,1,0:T(8,128)S(1)} %get-tuple-element.64.refs_0_) | copy-start | bytes 1585156
  58.2 15.4 %collective-permute-start.9 = (f32[1,129,8,128]{3,2,1,0:T(8,128)S(1)}, f32[1,129,8,128]{3,2,1,0:T(8,128)S(1)}, u32[]{:S(2)}, u32[]{:S(2)}) collective-permute-start(f32[1,129,8,128]{3,2,1,0:T(8,128)S(1)} %get-tuple-element.65), channel_id=1, source_target_pairs={{0,16},{1,65},{2,18},{3,67},{4,20},{5,69},{6,22},{7,71},{8,24},{9,... | collective-permute-start | bytes 1585160 | tf_op jit(solution)/shard_map/ppermute | solution.py:695
  64.3 13.3 %copy-start.15 = (s32[1,8,32]{2,1,0:T(8,128)S(1)}, s32[1,8,32]{2,1,0:T(8,128)}, u32[]{:S(2)}) copy-start(s32[1,8,32]{2,1,0:T(8,128)} %param.15) | copy-start | bytes 3076
  64.3 13.4 %copy-start.16 = (s32[1,8,32]{2,1,0:T(8,128)S(1)}, s32[1,8,32]{2,1,0:T(8,128)}, u32[]{:S(2)}) copy-start(s32[1,8,32]{2,1,0:T(8,128)} %param.14) | copy-start | bytes 3076
  64.3 13.4 %copy-start.17 = (f32[16,2]{0,1:T(2,128)S(1)}, f32[16,2]{0,1:T(2,128)}, u32[]{:S(2)}) copy-start(f32[16,2]{0,1:T(2,128)} %param.18) | copy-start | bytes 388
  64.3 13.5 %copy-start.12 = (f32[4,8,128]{2,1,0:T(8,128)S(1)}, f32[4,8,128]{2,1,0:T(8,128)}, u32[]{:S(2)}) copy-start(f32[4,8,128]{2,1,0:T(8,128)} %constant.71) | copy-start | bytes 49156
  64.3 13.5 %copy-start.13 = (f32[4,8,128]{2,1,0:T(8,128)S(1)}, f32[4,8,128]{2,1,0:T(8,128)}, u32[]{:S(2)}) copy-start(f32[4,8,128]{2,1,0:T(8,128)} %constant.69) | copy-start | bytes 49156
  64.3 13.5 %copy-start.14 = (f32[4,8,128]{2,1,0:T(8,128)S(1)}, f32[4,8,128]{2,1,0:T(8,128)}, u32[]{:S(2)}) copy-start(f32[4,8,128]{2,1,0:T(8,128)} %constant.67) | copy-start | bytes 49156
  64.3 14.6 %copy-start.10 = (s32[1,256]{1,0:T(1,128)S(1)}, s32[1,256]{1,0:T(1,128)}, u32[]{:S(2)}) copy-start(s32[1,256]{1,0:T(1,128)} %param.16) | copy-start | bytes 3076
  64.3 14.6 %copy-start.11 = (s32[1,32]{1,0:T(1,128)S(1)}, s32[1,32]{1,0:T(1,128)}, u32[]{:S(2)}) copy-start(s32[1,32]{1,0:T(1,128)} %param.17) | copy-start | bytes 388
  68.8 34.1 %collective-permute-start.14 = (f32[257,8,128]{2,1,0:T(8,128)}, f32[257,8,128]{2,1,0:T(8,128)S(1)}, u32[]{:S(2)}, u32[]{:S(2)}) collective-permute-start(f32[257,8,128]{2,1,0:T(8,128)} %gather.6), channel_id=1, source_target_pairs={{0,96},{1,25},{2,98},{3,27},{4,100},{5,29},{6,102},{7,31},{8,104},... | collective-permute-start | bytes 3158024 | tf_op jit(solution)/shard_map/ppermute | solution.py:695
  69.5 33.3 %collective-permute-start.12 = (f32[257,8,128]{2,1,0:T(8,128)}, f32[257,8,128]{2,1,0:T(8,128)S(1)}, u32[]{:S(2)}, u32[]{:S(2)}) collective-permute-start(f32[257,8,128]{2,1,0:T(8,128)} %gather.5), channel_id=1, source_target_pairs={{0,32},{1,9},{2,34},{3,11},{4,36},{5,13},{6,38},{7,15},{8,40},{9,1... | collective-permute-start | bytes 3158024 | tf_op jit(solution)/shard_map/ppermute | solution.py:695
  70.9 32.0 %collective-permute-start.13 = (f32[257,8,128]{2,1,0:T(8,128)}, f32[257,8,128]{2,1,0:T(8,128)S(1)}, u32[]{:S(2)}, u32[]{:S(2)}) collective-permute-start(f32[257,8,128]{2,1,0:T(8,128)} %gather.4), channel_id=1, source_target_pairs={{0,64},{1,17},{2,66},{3,19},{4,68},{5,21},{6,70},{7,23},{8,72},{9,... | collective-permute-start | bytes 3158024 | tf_op jit(solution)/shard_map/ppermute | solution.py:695
  73.5 26.1 %collective-permute-start.10 = (f32[1,129,8,128]{3,2,1,0:T(8,128)}, f32[1,129,8,128]{3,2,1,0:T(8,128)}, u32[]{:S(2)}, u32[]{:S(2)}) collective-permute-start(f32[1,129,8,128]{3,2,1,0:T(8,128)} %get-tuple-element.66), channel_id=1, source_target_pairs={{0,8},{1,33},{2,10},{3,35},{4,12},{5,37},{6,14},{7,39},{8,16},{9,4... | collective-permute-start | bytes 1585160 | tf_op jit(solution)/shard_map/ppermute | solution.py:695
  73.5 0.8 copy-start.4
  74.3 25.3 %collective-permute-start.11 = (f32[1,129,8,128]{3,2,1,0:T(8,128)}, f32[1,129,8,128]{3,2,1,0:T(8,128)}, u32[]{:S(2)}, u32[]{:S(2)}) collective-permute-start(f32[1,129,8,128]{3,2,1,0:T(8,128)} %get-tuple-element.67), channel_id=1, source_target_pairs={{0,24},{1,97},{2,26},{3,99},{4,28},{5,101},{6,30},{7,103},{8,0},{9... | collective-permute-start | bytes 1585160 | tf_op jit(solution)/shard_map/ppermute | solution.py:695
  77.7 21.9 %copy-start.3 = (f32[1,129,8,128]{3,2,1,0:T(8,128)S(1)}, f32[1,129,8,128]{3,2,1,0:T(8,128)}, u32[]{:S(2)}) copy-start(f32[1,129,8,128]{3,2,1,0:T(8,128)} %copy-done.2) | copy-start | bytes 1585156
  77.7 21.9 %copy-start.5 = (f32[1,129,8,128]{3,2,1,0:T(8,128)S(1)}, f32[1,129,8,128]{3,2,1,0:T(8,128)}, u32[]{:S(2)}) copy-start(f32[1,129,8,128]{3,2,1,0:T(8,128)} %copy-done.4) | copy-start | bytes 1585156
  82.7 20.2 %copy-start.6 = (bf16[4,256,256]{2,1,0:T(8,128)(2,1)S(1)}, bf16[4,256,256]{2,1,0:T(8,128)(2,1)}, u32[]{:S(2)}) copy-start(bf16[4,256,256]{2,1,0:T(8,128)(2,1)} %constant.60.clone.both) | copy-start | bytes 1572868
  82.7 20.2 %copy-start.7 = (f32[2,8,8,128]{3,2,1,0:T(8,128)S(1)}, f32[2,8,8,128]{3,2,1,0:T(8,128)}, u32[]{:S(2)}) copy-start(f32[2,8,8,128]{3,2,1,0:T(8,128)} %constant.61.clone.rows) | copy-start | bytes 196612
  109.9 2.1 %collective-permute-start.15 = (f32[4,36,8,128]{3,2,1,0:T(8,128)S(1)}, f32[4,36,8,128]{3,2,1,0:T(8,128)S(1)}, u32[]{:S(2)}, u32[]{:S(2)}) collective-permute-start(f32[4,36,8,128]{3,2,1,0:T(8,128)S(1)} %get-tuple-element.74), channel_id=1, source_target_pairs={{0,1},{1,0},{2,3},{3,2},{4,5},{5,4},{6,7},{7,6},{8,9},{9,8},{10,11... | collective-permute-start | bytes 1769480 | tf_op jit(solution)/shard_map/ppermute | solution.py:801
  112.1 10.6 %collective-permute-start.18 = (f32[36,8,128]{2,1,0:T(8,128)S(1)}, f32[36,8,128]{2,1,0:T(8,128)S(1)}, u32[]{:S(2)}, u32[]{:S(2)}) collective-permute-start(f32[36,8,128]{2,1,0:T(8,128)S(1)} %get-tuple-element.79), channel_id=1, source_target_pairs={{0,6},{1,7},{2,0},{3,1},{4,2},{5,3},{6,4},{7,5},{8,14},{9,15},{10,... | collective-permute-start | bytes 442376 | tf_op jit(solution)/shard_map/ppermute | solution.py:700
  116.1 8.2 %collective-permute-start.17 = (f32[36,8,128]{2,1,0:T(8,128)S(1)}, f32[36,8,128]{2,1,0:T(8,128)S(1)}, u32[]{:S(2)}, u32[]{:S(2)}) collective-permute-start(f32[36,8,128]{2,1,0:T(8,128)S(1)} %get-tuple-element.80), channel_id=1, source_target_pairs={{0,4},{1,5},{2,6},{3,7},{4,0},{5,1},{6,2},{7,3},{8,12},{9,13},{10,... | collective-permute-start | bytes 442376 | tf_op jit(solution)/shard_map/ppermute | solution.py:700
  117.2 9.2 %collective-permute-start.16 = (f32[36,8,128]{2,1,0:T(8,128)S(1)}, f32[36,8,128]{2,1,0:T(8,128)S(1)}, u32[]{:S(2)}, u32[]{:S(2)}) collective-permute-start(f32[36,8,128]{2,1,0:T(8,128)S(1)} %get-tuple-element.81), channel_id=1, source_target_pairs={{0,2},{1,3},{2,4},{3,5},{4,6},{5,7},{6,0},{7,1},{8,10},{9,11},{10,... | collective-permute-start | bytes 442376 | tf_op jit(solution)/shard_map/ppermute | solution.py:700
